TPU v7x, 32 devices: a whole 2x2x4 slice. The times are simulated.
32 devices in a mesh: section: 2 (over x), fsdp: 4 (over y, core), rep: 4 (over z).
Axes of the slice: x: 2, y: 2, z: 4, core: 2. Of those that a mesh axis runs over, the one named last changes fastest.
Arguments:
- inputs: float32 [32, 512, 1536], P(('fsdp', 'rep')), may hold values from -6 to 6
- cotangent: float32 [32, 512, 1536], P(('fsdp', 'rep')), may hold values from -6 to 6
- doc_ids: int32 [32, 512], P(('fsdp', 'rep')), may hold values from 0 to 3, never falling along the last dimension, each value on 1 to 256 neighbouring positions
- in_weight: bfloat16 [2, 1536, 6448], P('section', 'fsdp'), may hold values from -0.15625 to 0.15625
- out_weight: bfloat16 [2, 3072, 1536], P('section', 'fsdp'), may hold values from -0.109375 to 0.109375
- conv_weight: bfloat16 [2, 3328, 4], P('section', 'fsdp'), may hold values from -3 to 3
- conv_bias: bfloat16 [2, 3328], P('section', 'fsdp'), may hold values from -0.5 to 0.5
- step_bias: bfloat16 [2, 48], P('section', 'fsdp'), may hold values from -6.875 to -2.296875
- decay_log: bfloat16 [2, 48], P('section', 'fsdp'), may hold values from 0 to 2.765625
- skip_gain: bfloat16 [2, 48], P('section', 'fsdp'), may hold values from 0.5 to 1.5
- pre_gain: bfloat16 [2, 1536], P('section', 'fsdp'), may hold values from 0.5 to 1.5
- mix_gain: bfloat16 [2, 3072], P('section', 'fsdp'), may hold values from 0.5 to 1.5
Outputs:
- section_out: float32 [2, 32, 512, 1536], P('section', ('fsdp', 'rep'))
- section_in_grad: float32 [2, 32, 512, 1536], P('section', ('fsdp', 'rep'))
- grad_in_weight: float32 [2, 1536, 6448], P('section', 'fsdp')
- grad_out_weight: float32 [2, 3072, 1536], P('section', 'fsdp')
- grad_conv_weight: float32 [2, 3328, 4], P('section', 'fsdp')
- grad_conv_bias: float32 [2, 3328], P('section', 'fsdp')
- grad_step_bias: float32 [2, 48], P('section', 'fsdp')
- grad_decay_log: float32 [2, 48], P('section', 'fsdp')
- grad_skip_gain: float32 [2, 48], P('section', 'fsdp')
- grad_pre_gain: float32 [2, 1536], P('section', 'fsdp')
- grad_mix_gain: float32 [2, 3072], P('section', 'fsdp')
Inputs may be any that keep to these rules, and one draw needn't show every extreme that they name: Along each sequence doc_ids never fall; each run of equal numbers is one document of 1 to 256 tokens, at most 4 documents a sequence, and some document has exactly 256.
All inputs are finite; a program needn't handle non-finite values.
Results may differ from a plain program's by a relative error of at most 0.017.
Values may be sent and summed in bfloat16 or wider, within the bound.
No kernel may reach another device: no remote copies, remote signals or barrier semaphores. Data moves between devices by JAX's collectives and lax.ppermute only.
A program may use at most 832 MiB of HBM per device.

v0:
```python
import jax
import jax.numpy as jnp
from jax import lax
from jax.sharding import PartitionSpec as P

BLOCK = 256


HIGHEST = lax.Precision.HIGHEST
EPS = 1e-05


def shifted_2(value, axis, steps):
    count = lax.axis_size(axis)
    initial, last = (max(0, -steps), min(count, count - steps))
    return lax.ppermute(value, axis, [(source, source + steps) for source in range(initial, last)])


def prenorm(hidden, gain):
    return hidden * lax.rsqrt(jnp.mean(hidden * hidden, -1, keepdims=True) + EPS) * gain


def block_scan(scaled, input_map, output_map, log_decay, doc_ids):
    length, head_count, head_width = scaled.shape
    block_count = length // BLOCK
    values = scaled.reshape(block_count, BLOCK, head_count, head_width)
    in_rows = input_map.reshape(block_count, BLOCK, -1)
    out_rows = output_map.reshape(block_count, BLOCK, -1)
    totals = jnp.swapaxes(
        jnp.cumsum(log_decay.reshape(block_count, BLOCK, head_count), axis=1), 1, 2
    )
    doc_blocks = doc_ids.reshape(block_count, BLOCK)
    later_pos = lax.broadcasted_iota(jnp.int32, (BLOCK, BLOCK), 0)
    earlier_pos = lax.broadcasted_iota(jnp.int32, (BLOCK, BLOCK), 1)
    same_doc = (doc_blocks[:, :, None] == doc_blocks[:, None, :]) & (earlier_pos <= later_pos)
    span_logs = totals[:, :, :, None] - totals[:, :, None, :]
    decays = jnp.exp(jnp.where(same_doc[:, None], span_logs, -jnp.inf))
    scores = jnp.einsum("btn,bsn->bts", out_rows, in_rows, precision=HIGHEST)
    inner_part = jnp.einsum("bhts,bshp->bthp", decays * scores[:, None], values, precision=HIGHEST)
    end_logs = totals[:, :, -1:]
    to_end = (
        jnp.exp(end_logs - totals)
        * (doc_blocks == doc_blocks[:, -1:]).astype(jnp.float32)[:, None, :]
    )
    states = jnp.einsum("bsn,bhs,bshp->bhnp", in_rows, to_end, values, precision=HIGHEST)
    entering = [jnp.zeros_like(states[0])]
    running = states[0]
    entering.append(running)
    entered = jnp.stack(entering)
    previous_end = jnp.concatenate([doc_blocks[:1, -1:], doc_blocks[:-1, -1:]], 0)
    from_start = jnp.exp(totals) * (doc_blocks == previous_end).astype(jnp.float32)[:, None, :]
    outer_part = jnp.einsum("btn,bht,bhnp->bthp", out_rows, from_start, entered, precision=HIGHEST)
    return (inner_part + outer_part).reshape(length, head_count, head_width)


def mixer(projected, doc_ids, conv_weight, conv_bias, step_bias, decay_log, skip_gain, mix_gain):
    length = projected.shape[0]
    inner_width = mix_gain.shape[0]
    channels = conv_weight.shape[0]
    tap_count = conv_weight.shape[1]
    state_width = (channels - inner_width) // 2
    head_count = decay_log.shape[0]
    gate_part = projected[:, :inner_width]
    conv_in = projected[:, inner_width : inner_width + channels]
    step_raw = projected[:, inner_width + channels :]
    conv_out = conv_bias + conv_weight[:, tap_count - 1] * conv_in
    for offset in range(1, tap_count):
        shifted = jnp.pad(conv_in[: length - offset], ((offset, 0), (0, 0)))
        shifted_ids = jnp.pad(doc_ids[: length - offset], (offset, 0), constant_values=-1)
        same_doc = (shifted_ids == doc_ids).astype(jnp.float32)[:, None]
        conv_out = conv_out + conv_weight[:, tap_count - 1 - offset] * shifted * same_doc
    activated = jax.nn.silu(conv_out)
    values = activated[:, :inner_width].reshape(length, head_count, inner_width // head_count)
    input_map = activated[:, inner_width : inner_width + state_width]
    output_map = activated[:, inner_width + state_width :]
    step_size = jax.nn.softplus(step_raw + step_bias)
    log_decay = -jnp.exp(decay_log) * step_size
    scanned = block_scan(values * step_size[:, :, None], input_map, output_map, log_decay, doc_ids)
    gated = (scanned + skip_gain[:, None] * values).reshape(length, inner_width) * jax.nn.silu(
        gate_part
    )
    return gated * lax.rsqrt(jnp.mean(gated * gated, -1, keepdims=True) + EPS) * mix_gain


def store_slot(buffer, update, slot_index, active):
    previous = lax.dynamic_index_in_dim(buffer, slot_index, 0, keepdims=False)
    return lax.dynamic_update_index_in_dim(
        buffer, jnp.where(active, update, previous), slot_index, 0
    )


def add_terms(first, second):
    return tuple((left + right for left, right in zip(first, second)))


def per_device(
    inputs,
    cotangent,
    doc_ids,
    in_weight,
    out_weight,
    conv_weight,
    conv_bias,
    step_bias,
    decay_log,
    skip_gain,
    pre_gain,
    mix_gain,
):
    section_id = lax.axis_index("section")
    section_count = lax.axis_size("section")
    micro_count, length, model_width = inputs.shape
    proj_width = in_weight.shape[2]
    tick_count = micro_count + section_count - 1
    gathered = (
        lax.all_gather(in_weight, "fsdp", axis=1, tiled=True),
        lax.all_gather(out_weight, "fsdp", axis=1, tiled=True),
        lax.all_gather(conv_weight, "fsdp", axis=1, tiled=True),
        lax.all_gather(conv_bias, "fsdp", axis=1, tiled=True),
        lax.all_gather(step_bias, "fsdp", axis=1, tiled=True),
        lax.all_gather(decay_log, "fsdp", axis=1, tiled=True),
        lax.all_gather(skip_gain, "fsdp", axis=1, tiled=True),
        lax.all_gather(pre_gain, "fsdp", axis=1, tiled=True),
        lax.all_gather(mix_gain, "fsdp", axis=1, tiled=True),
    )
    forward_weights = tuple((weight_piece[0] for weight_piece in gathered))
    forward_small = [weight_piece.astype(jnp.float32) for weight_piece in forward_weights[2:]]

    def forward(hidden, tick_ids):
        normed = prenorm(hidden, forward_small[5]).astype(jnp.bfloat16)
        projected = jnp.dot(normed, forward_weights[0], preferred_element_type=jnp.float32)
        mixed = mixer(
            projected,
            tick_ids,
            forward_small[0],
            forward_small[1],
            forward_small[2],
            forward_small[3],
            forward_small[4],
            forward_small[6],
        ).astype(jnp.bfloat16)
        return (
            hidden + jnp.dot(mixed, forward_weights[1], preferred_element_type=jnp.float32),
            projected,
        )

    def spare_forward(hidden, tick_ids):
        return (jnp.zeros_like(hidden), jnp.zeros((length, proj_width), jnp.float32))

    kept_in = jnp.zeros((micro_count, length, model_width), jnp.float32)
    kept_proj = jnp.zeros((micro_count, length, proj_width), jnp.float32)
    outputs = jnp.zeros((micro_count, length, model_width), jnp.float32)
    arrived = jnp.zeros((length, model_width), jnp.bfloat16)
    for tick_index in range(tick_count):
        position = tick_index - section_id
        active = (position >= 0) & (position < micro_count)
        slot_index = jnp.clip(position, 0, micro_count - 1)
        own_rows = lax.dynamic_index_in_dim(inputs, slot_index, 0, keepdims=False)
        tick_ids = lax.dynamic_index_in_dim(doc_ids, slot_index, 0, keepdims=False)
        hidden = jnp.where(section_id == 0, own_rows, arrived.astype(jnp.float32))
        result, projected = lax.cond(active, forward, spare_forward, hidden, tick_ids)
        kept_in = store_slot(kept_in, hidden, slot_index, active)
        kept_proj = store_slot(kept_proj, projected, slot_index, active)
        outputs = store_slot(outputs, result, slot_index, active)
        arrived = shifted_2(result.astype(jnp.bfloat16), "section", 1)
    regathered = (
        lax.all_gather(in_weight, "fsdp", axis=1, tiled=True),
        lax.all_gather(out_weight, "fsdp", axis=1, tiled=True),
        lax.all_gather(conv_weight, "fsdp", axis=1, tiled=True),
        lax.all_gather(conv_bias, "fsdp", axis=1, tiled=True),
        lax.all_gather(step_bias, "fsdp", axis=1, tiled=True),
        lax.all_gather(decay_log, "fsdp", axis=1, tiled=True),
        lax.all_gather(skip_gain, "fsdp", axis=1, tiled=True),
        lax.all_gather(pre_gain, "fsdp", axis=1, tiled=True),
        lax.all_gather(mix_gain, "fsdp", axis=1, tiled=True),
    )
    backward_weights = tuple((weight_piece[0] for weight_piece in regathered))
    backward_small = [weight_piece.astype(jnp.float32) for weight_piece in backward_weights[2:]]
    term_shapes = [weight_piece.shape for weight_piece in backward_weights]
    contract_rows = (((0,), (0,)), ((), ()))
    contract_cols = (((1,), (1,)), ((), ()))

    def backward(upstream, hidden, projected, tick_ids):
        upstream_low = upstream.astype(jnp.bfloat16)
        normed, norm_back = jax.vjp(prenorm, hidden, backward_small[5])
        normed_low = normed.astype(jnp.bfloat16)

        def core_part(proj_in, conv_w, conv_b, step_b, decay_l, skip_g, mix_g):
            return mixer(proj_in, tick_ids, conv_w, conv_b, step_b, decay_l, skip_g, mix_g)

        mixed, core_back = jax.vjp(
            core_part,
            projected,
            backward_small[0],
            backward_small[1],
            backward_small[2],
            backward_small[3],
            backward_small[4],
            backward_small[6],
        )
        mixed_low = mixed.astype(jnp.bfloat16)
        out_term = lax.dot_general(
            mixed_low, upstream_low, contract_rows, preferred_element_type=jnp.float32
        )
        mixed_grad = lax.dot_general(
            upstream_low, backward_weights[1], contract_cols, preferred_element_type=jnp.float32
        )
        proj_grad, conv_w_grad, conv_b_grad, step_grad, decay_grad, skip_grad, mix_grad = core_back(
            mixed_grad
        )
        proj_low = proj_grad.astype(jnp.bfloat16)
        in_term = lax.dot_general(
            normed_low, proj_low, contract_rows, preferred_element_type=jnp.float32
        )
        normed_grad = lax.dot_general(
            proj_low, backward_weights[0], contract_cols, preferred_element_type=jnp.float32
        )
        hidden_grad, pre_grad = norm_back(normed_grad)
        return (
            upstream + hidden_grad,
            (
                in_term,
                out_term,
                conv_w_grad,
                conv_b_grad,
                step_grad,
                decay_grad,
                skip_grad,
                pre_grad,
                mix_grad,
            ),
        )

    def spare_backward(upstream, hidden, projected, tick_ids):
        return (
            jnp.zeros_like(upstream),
            tuple((jnp.zeros(shape_one, jnp.float32) for shape_one in term_shapes)),
        )

    in_grads = jnp.zeros((micro_count, length, model_width), jnp.float32)
    coming = jnp.zeros((length, model_width), jnp.bfloat16)
    totals = tuple((jnp.zeros(shape_one, jnp.float32) for shape_one in term_shapes))
    for tick_index in range(tick_count):
        position = tick_index - (section_count - 1 - section_id)
        active = (position >= 0) & (position < micro_count)
        slot_index = jnp.clip(position, 0, micro_count - 1)
        own_rows = lax.dynamic_index_in_dim(cotangent, slot_index, 0, keepdims=False)
        upstream = jnp.where(section_id == section_count - 1, own_rows, coming.astype(jnp.float32))
        hidden = lax.dynamic_index_in_dim(kept_in, slot_index, 0, keepdims=False)
        projected = lax.dynamic_index_in_dim(kept_proj, slot_index, 0, keepdims=False)
        tick_ids = lax.dynamic_index_in_dim(doc_ids, slot_index, 0, keepdims=False)
        hidden_grad, terms = lax.cond(
            active, backward, spare_backward, upstream, hidden, projected, tick_ids
        )
        in_grads = store_slot(in_grads, hidden_grad, slot_index, active)
        totals = add_terms(totals, terms)
        coming = shifted_2(hidden_grad.astype(jnp.bfloat16), "section", -1)
    totals = (
        lax.psum_scatter(
            totals[0].astype(jnp.bfloat16), "fsdp", scatter_dimension=0, tiled=True
        ).astype(jnp.float32),
        lax.psum_scatter(
            totals[1].astype(jnp.bfloat16), "fsdp", scatter_dimension=0, tiled=True
        ).astype(jnp.float32),
        lax.psum_scatter(
            totals[2].astype(jnp.bfloat16), "fsdp", scatter_dimension=0, tiled=True
        ).astype(jnp.float32),
        lax.psum_scatter(
            totals[3].astype(jnp.bfloat16), "fsdp", scatter_dimension=0, tiled=True
        ).astype(jnp.float32),
        lax.psum_scatter(
            totals[4].astype(jnp.bfloat16), "fsdp", scatter_dimension=0, tiled=True
        ).astype(jnp.float32),
        lax.psum_scatter(
            totals[5].astype(jnp.bfloat16), "fsdp", scatter_dimension=0, tiled=True
        ).astype(jnp.float32),
        lax.psum_scatter(
            totals[6].astype(jnp.bfloat16), "fsdp", scatter_dimension=0, tiled=True
        ).astype(jnp.float32),
        lax.psum_scatter(
            totals[7].astype(jnp.bfloat16), "fsdp", scatter_dimension=0, tiled=True
        ).astype(jnp.float32),
        lax.psum_scatter(
            totals[8].astype(jnp.bfloat16), "fsdp", scatter_dimension=0, tiled=True
        ).astype(jnp.float32),
    )
    totals = (
        lax.psum(totals[0].astype(jnp.bfloat16), "rep").astype(jnp.float32),
        lax.psum(totals[1].astype(jnp.bfloat16), "rep").astype(jnp.float32),
        lax.psum(totals[2].astype(jnp.bfloat16), "rep").astype(jnp.float32),
        lax.psum(totals[3].astype(jnp.bfloat16), "rep").astype(jnp.float32),
        lax.psum(totals[4].astype(jnp.bfloat16), "rep").astype(jnp.float32),
        lax.psum(totals[5].astype(jnp.bfloat16), "rep").astype(jnp.float32),
        lax.psum(totals[6].astype(jnp.bfloat16), "rep").astype(jnp.float32),
        lax.psum(totals[7].astype(jnp.bfloat16), "rep").astype(jnp.float32),
        lax.psum(totals[8].astype(jnp.bfloat16), "rep").astype(jnp.float32),
    )
    return (
        outputs[None],
        in_grads[None],
        totals[0][None],
        totals[1][None],
        totals[2][None],
        totals[3][None],
        totals[4][None],
        totals[5][None],
        totals[6][None],
        totals[7][None],
        totals[8][None],
    )


def solution(mesh):
    return jax.shard_map(
        per_device,
        mesh=mesh,
        in_specs=(
            P(("fsdp", "rep"), None, None),
            P(("fsdp", "rep"), None, None),
            P(("fsdp", "rep"), None),
            P("section", "fsdp", None),
            P("section", "fsdp", None),
            P("section", "fsdp", None),
            P("section", "fsdp"),
            P("section", "fsdp"),
            P("section", "fsdp"),
            P("section", "fsdp"),
            P("section", "fsdp"),
            P("section", "fsdp"),
        ),
        out_specs=(
            P("section", ("fsdp", "rep"), None, None),
            P("section", ("fsdp", "rep"), None, None),
            P("section", "fsdp", None),
            P("section", "fsdp", None),
            P("section", "fsdp", None),
            P("section", "fsdp"),
            P("section", "fsdp"),
            P("section", "fsdp"),
            P("section", "fsdp"),
            P("section", "fsdp"),
            P("section", "fsdp"),
        ),
        check_vma=False,
    )
```

profile of v0, /device:TPU:0, one launch (start us, length us, event | category | flops | bytes accessed | tf_op | source)
XLA Modules:
  0.0 3027.7 jit_solution(3845025262336812757)
XLA Ops:
  34.4 23.3 all_gather.37
  73.8 12.3 all-gather.5.cloned.1.call-done
  86.1 128.7 %all-gather.3.cloned.1.call-done = bf16[1,1536,6448]{2,1,0:T(8,128)(2,1)} async-done(((bf16[1,384,6448]{2,1,0:T(8,128)(2,1)}), bf16[1,1536,6448]{2,1,0:T(8,128)(2,1)}) %all-gather.3.cloned.1.call-update) | async-done | bytes 19808272 | tf_op jit(solution)/shard_map/all_gather | solution.py:116
  217.1 169.1 %conditional.6 = (f32[512,1536]{1,0:T(8,128)}, f32[512,6448]{1,0:T(8,128)}) conditional(s32[]{:T(128)} %convert_element_type.439, () %tuple.89, (f32[1,512,1536]{2,1,0:T(8,128)}, pred[512,1536]{1,0:T(8,128)(4,1)S(1)}, f32[512,1536]{1,0:T(8,128)}, f32[3328]{0:T(1024)S(1)}, f32[3328,4]{1,0:T(8,128)S(1)}, /*index=5*/f32[1536]{0:T(1024)S(1)}, ...), branch_computations={%region_0.1_spmd, %region_1.6_spmd} | conditional | flops 24919117824 | bytes 445701888 | solution.py:161
  226.5 19.1 fusion.26
  310.8 29.2 bitcast_add_fusion
  371.9 13.9 copy.605
  441.2 166.2 %conditional.7 = (f32[512,1536]{1,0:T(8,128)}, f32[512,6448]{1,0:T(8,128)}) conditional(s32[]{:T(128)} %convert_element_type.454, () %tuple.91, (f32[3328]{0:T(1024)S(1)}, f32[3328,4]{1,0:T(8,128)S(1)}, f32[512,1536]{1,0:T(8,128)S(1)}, f32[1536]{0:T(1024)S(1)}, bf16[1536,6448]{1,0:T(8,128)(2,1)}, /*index=5*/s32[2,512]{1,0:T(2,128)S(1)}, s32[]{:T(128)}, ...), branch_computations={%region_6.7_spmd, %region_7.12_spmd} | conditional | flops 24918331392 | bytes 451206912 | solution.py:161
  443.1 18.9 fusion.63
  486.2 12.4 divide_multiply_fusion.1
  531.7 29.5 bitcast_add_fusion.1
  593.4 14.0 copy.607
  611.9 14.6 bitcast_dynamic-update-slice_fusion.1
  674.7 31.4 %conditional.9 = (f32[512,1536]{1,0:T(8,128)}, f32[1536,6448]{0,1:T(8,128)}, f32[3072,1536]{1,0:T(8,128)}, f32[3328,4]{0,1:T(4,128)}, f32[3328]{0:T(1024)}, /*in...) conditional(s32[]{:T(128)} %convert_element_type.460, () %tuple.95, ...), branch_computations={%region_18.19_spmd, %region_19.45_spmd} | conditional | flops 58643644416 | bytes 1163119744 | solution.py:252
  689.5 13.3 broadcast.874
  710.7 666.3 %collective-permute-done.2 = bf16[512,1536]{1,0:T(8,128)(2,1)} collective-permute-done((bf16[512,1536]{1,0:T(8,128)(2,1)}, bf16[512,1536]{1,0:T(8,128)(2,1)}, u32[]{:S(2)}, u32[]{:S(2)}) %collective-permute-start.2) | collective-permute-done | bytes 1572896 | tf_op jit(solution)/shard_map/ppermute | solution.py:16
  1380.5 503.0 %conditional.10 = (f32[512,1536]{1,0:T(8,128)}, f32[1536,6448]{0,1:T(8,128)}, f32[3072,1536]{1,0:T(8,128)}, f32[3328,4]{0,1:T(4,128)}, f32[3328]{0:T(1024)}, /*i...) conditional(s32[]{:T(128)} %convert_element_type.461, () %tuple.97, ...), branch_computations={%region_44.46_spmd, %region_45.71_spmd} | conditional | flops 58643644416 | bytes 1154075776 | solution.py:252
  1437.9 13.6 fusion.245
  1503.7 29.3 fusion.252
  1563.2 14.1 multiply_reduce_fusion.26
  1577.3 13.6 multiply_reduce_fusion.27
  1606.7 13.3 multiply_reduce_fusion.25
  1620.0 12.6 fusion.309
  1632.7 38.3 %fusion.232 = (f32[2,48,256]{2,1,0:T(8,128)S(1)}, f32[2,48,256]{2,1,0:T(8,128)}, f32[2,256,256]{2,1,0:T(8,128)S(1)}) fusion(f32[2,256,256]{2,1,0:T(8,128)S(1)} %copy-done.79, f32[2,48,256]{2,1,0:T(8,128)S(1)} %copy-done.90, pred[2,256,256]{2,1,0:T(8,128)(4,1)S(1)} %copy-done.125, f32[2,256,48,64]{1,3,2,0:T(8,128)} %copy.469, f32[2,256,48]{1,2,0:T(8,128)S(1)} %copy.468, ...), kind=kOutput, calls=%fused_computation.416 | convolution fusion | flops 4889853952 | bytes 14155776 | tf_op jit(solution)/shard_map/cond/branch_1_fun/transpose(jvp(bhts,bshp->bthp))/dot_general | solution.py:39
  1694.8 22.1 bitcast_add_fusion.4
  1819.5 13.5 fusion.457
  1833.1 19.8 multiply_reduce_fusion.31
  1861.1 22.4 fusion.301
  1888.2 36.3 %collective-permute-done.3 = bf16[512,1536]{1,0:T(8,128)(2,1)} collective-permute-done((bf16[512,1536]{1,0:T(8,128)(2,1)}, bf16[512,1536]{1,0:T(8,128)(2,1)}, u32[]{:S(2)}, u32[]{:S(2)}) %collective-permute-start.3) | collective-permute-done | bytes 1572896 | tf_op jit(solution)/shard_map/ppermute | solution.py:16
  1928.1 503.9 %conditional.11 = (f32[512,1536]{1,0:T(8,128)}, f32[1536,6448]{0,1:T(8,128)}, f32[3072,1536]{1,0:T(8,128)}, f32[3328,4]{0,1:T(4,128)}, f32[3328]{0:T(1024)}, /*i...) conditional(s32[]{:T(128)} %convert_element_type.464, () %tuple.99, ...), branch_computations={%region_70.72_spmd, %region_71.97_spmd} | conditional | flops 58643644416 | bytes 1153684096 | solution.py:252
  1985.5 13.5 fusion.360
  2051.3 29.2 fusion.367
  2110.6 14.0 multiply_reduce_fusion.39
  2124.7 13.6 multiply_reduce_fusion.40
  2154.0 13.3 multiply_reduce_fusion.38
  2167.3 12.7 fusion.424
  2180.0 38.3 %fusion.347 = (f32[2,48,256]{2,1,0:T(8,128)S(1)}, f32[2,48,256]{2,1,0:T(8,128)}, f32[2,256,256]{2,1,0:T(8,128)S(1)}) fusion(f32[2,256,256]{2,1,0:T(8,128)S(1)} %copy-done.82, f32[2,48,256]{2,1,0:T(8,128)S(1)} %copy-done.93, pred[2,256,256]{2,1,0:T(8,128)(4,1)S(1)} %copy-done.127, f32[2,256,48,64]{1,3,2,0:T(8,128)} %copy.493, f32[2,256,48]{1,2,0:T(8,128)S(1)} %copy.492, ...), kind=kOutput, calls=%fused_computation.599 | convolution fusion | flops 4889853952 | bytes 14155776 | tf_op jit(solution)/shard_map/cond/branch_1_fun/transpose(jvp(bhts,bshp->bthp))/dot_general | solution.py:39
  2242.3 22.3 bitcast_add_fusion.5
  2367.2 13.5 fusion.458
  2380.7 20.3 multiply_reduce_fusion.44
  2409.2 22.6 fusion.416
  2432.0 43.9 %add_convert_fusion.9 = bf16[1536,6448]{0,1:T(8,128)(2,1)} fusion(f32[1536,6448]{0,1:T(8,128)} %get-tuple-element.673, f32[1536,6448]{0,1:T(8,128)} %get-tuple-element.671, f32[1536,6448]{0,1:T(8,128)} %get-tuple-element.672), kind=kLoop, calls=%fused_computation.775 | loop fusion | flops 29712384 | bytes 138657792 | tf_op jit(solution)/shard_map/convert_element_type | solution.py:260
  2475.9 24.5 copy.600
  2500.5 31.6 %add_convert_fusion.10 = bf16[3072,1536]{1,0:T(8,128)(2,1)} fusion(f32[3072,1536]{1,0:T(8,128)} %get-tuple-element.676, f32[3072,1536]{1,0:T(8,128)} %get-tuple-element.674, f32[3072,1536]{1,0:T(8,128)} %get-tuple-element.675), kind=kLoop, calls=%fused_computation.776 | loop fusion | flops 14155776 | bytes 66060288 | tf_op jit(solution)/shard_map/convert_element_type | solution.py:263
  2534.4 110.3 %reduce-scatter.10.cloned.1.call-done = bf16[384,6448]{1,0:T(8,128)(2,1)} async-done(((bf16[1536,6448]{1,0:T(8,128)(2,1)}), bf16[384,6448]{1,0:T(8,128)(2,1)}) %reduce-scatter.10.cloned.1.call-update) | async-done | bytes 4952080
  2652.3 73.4 %reduce-scatter.8.cloned.1.call-done = bf16[768,1536]{1,0:T(8,128)(2,1)} async-done(((bf16[3072,1536]{1,0:T(8,128)(2,1)}), bf16[768,1536]{1,0:T(8,128)(2,1)}) %reduce-scatter.8.cloned.1.call-update) | async-done | bytes 2359312 | tf_op jit(solution)/shard_map/reduce_scatter | solution.py:262
  2770.1 23.9 all-reduce.97
  2797.9 213.5 %all-reduce.103.cloned.1.call-done = (bf16[1,384,6448]{1,2,0:T(8,128)(2,1)}, bf16[1,768,1536]{2,1,0:T(8,128)(2,1)}) async-done(((bf16[1,384,6448]{1,2,0:T(8,128)(2,1)}, bf16[1,768,1536]{2,1,0:T(8,128)(2,1)}), (bf16[1,384,6448]{1,2,0:T(8,128)(2,1)}, bf16[1,768,1536]{2,1,0:T(8,128)(2,1)})) %all-reduce.103.cloned.1.call-update) | async-done | bytes 7311376 | tf_op jit(solution)/shard_map/psum | solution.py:288
  (856 shorter events, 1030.6 us)
Async XLA Ops:
  7.2 79.0 %all-gather.5.cloned.1.call-start = ((), (), s32[]{:S(2)}) async-start(), calls=%async_computation.4 | async-start | bytes 11796480 | tf_op jit(solution)/shard_map/all_gather | solution.py:117
  8.0 206.9 %all-gather.3.cloned.1.call-start = ((), (), s32[]{:S(2)}) async-start(), calls=%async_computation.3 | async-start | bytes 25067520 | tf_op jit(solution)/shard_map/all_gather | solution.py:116
  15.6 43.9 %copy-start.205 = (bf16[1,384]{1,0:T(2,128)(2,1)S(1)}, bf16[1,384]{1,0:T(2,128)(2,1)}, u32[]{:S(2)}) copy-start(bf16[1,384]{1,0:T(2,128)(2,1)} %param.35) | copy-start | bytes 2308
  15.6 2629.2 %reduce-scatter.10.cloned.1.call-start = ((), (), s32[]{:S(2)}) async-start(), calls=%async_computation.6 | async-start | bytes 25067520
  28.1 188.9 %copy-start.214 = (f32[48]{0:T(128)}, f32[48]{0:T(128)S(1)}, u32[]{:S(2)}) copy-start(f32[48]{0:T(128)S(1)} %convert_element_type.485) | copy-start | bytes 580
  28.2 188.9 %copy-start.170 = (f32[48]{0:T(128)}, f32[48]{0:T(128)S(1)}, u32[]{:S(2)}) copy-start(f32[48]{0:T(128)S(1)} %convert_element_type.486) | copy-start | bytes 580
  28.2 645.6 %copy-start.69 = (f32[3328]{0:T(1024)}, f32[3328]{0:T(1024)S(1)}, u32[]{:S(2)}) copy-start(f32[3328]{0:T(1024)S(1)} %convert_element_type.483) | copy-start | bytes 39940
  59.5 614.3 %copy-start.3 = (f32[1,3328,4]{2,0,1:T(1,128)}, f32[1,3328,4]{2,0,1:T(1,128)S(1)}, u32[]{:S(2)}) copy-start(f32[1,3328,4]{2,0,1:T(1,128)S(1)} %convert_element_type.477) | copy-start | bytes 159748
  64.9 586.0 %copy-start.118 = (f32[1536]{0:T(1024)}, f32[1536]{0:T(1024)S(1)}, u32[]{:S(2)}) copy-start(f32[1536]{0:T(1024)S(1)} %convert_reduce_fusion) | copy-start | bytes 18436
  68.4 148.7 %copy-start.72 = (s32[2,512]{1,0:T(2,128)S(1)}, s32[2,512]{1,0:T(2,128)}, u32[]{:S(2)}) copy-start(s32[2,512]{1,0:T(2,128)} %param.27) | copy-start | bytes 12292
  395.6 39.8 %collective-permute-start = (bf16[512,1536]{1,0:T(8,128)(2,1)S(1)}, bf16[512,1536]{1,0:T(8,128)(2,1)}, u32[]{:S(2)}, u32[]{:S(2)}) collective-permute-start(bf16[512,1536]{1,0:T(8,128)(2,1)S(1)} %convert_element_type.455), channel_id=1, source_target_pairs={{0,16},{1,17},{2,18},{3,19},{4,20},{5,21},{6,22},{7,23},{8,24},{9,... | collective-permute-start | bytes 4718600 | tf_op jit(solution)/shard_map/ppermute | solution.py:16
  609.4 35.6 %collective-permute-start.1 = (bf16[512,1536]{1,0:T(8,128)(2,1)S(1)}, bf16[512,1536]{1,0:T(8,128)(2,1)}, u32[]{:S(2)}, u32[]{:S(2)}) collective-permute-start(bf16[512,1536]{1,0:T(8,128)(2,1)S(1)} %convert_element_type.458), channel_id=1, source_target_pairs={{0,16},{1,17},{2,18},{3,19},{4,20},{5,21},{6,22},{7,23},{8,24},{9,... | collective-permute-start | bytes 4718600 | tf_op jit(solution)/shard_map/ppermute | solution.py:16
  706.0 674.4 %copy-start.4 = (f32[1,3328,4]{2,0,1:T(1,128)S(1)}, f32[1,3328,4]{2,0,1:T(1,128)}, u32[]{:S(2)}) copy-start(f32[1,3328,4]{2,0,1:T(1,128)} %copy-done.3) | copy-start | bytes 159748
  706.1 674.4 %copy-start.15 = (pred[512,1536]{1,0:T(8,128)(4,1)S(1)}, pred[512,1536]{1,0:T(8,128)(4,1)}, u32[]{:S(2)}) copy-start(pred[512,1536]{1,0:T(8,128)(4,1)} %copy-done.14) | copy-start | bytes 2359300
  706.1 674.4 %copy-start.70 = (f32[3328]{0:T(1024)S(1)}, f32[3328]{0:T(1024)}, u32[]{:S(2)}) copy-start(f32[3328]{0:T(1024)} %copy-done.69) | copy-start | bytes 39940
  706.1 674.4 %copy-start.73 = (s32[2,512]{1,0:T(2,128)S(1)}, s32[2,512]{1,0:T(2,128)}, u32[]{:S(2)}) copy-start(s32[2,512]{1,0:T(2,128)} %param.27) | copy-start | bytes 12292
  706.1 674.4 %copy-start.218 = (f32[48]{0:T(128)S(1)}, f32[48]{0:T(128)}, u32[]{:S(2)}) copy-start(f32[48]{0:T(128)} %copy-done.214) | copy-start | bytes 580
  709.5 667.5 %collective-permute-start.2 = (bf16[512,1536]{1,0:T(8,128)(2,1)}, bf16[512,1536]{1,0:T(8,128)(2,1)}, u32[]{:S(2)}, u32[]{:S(2)}) collective-permute-start(bf16[512,1536]{1,0:T(8,128)(2,1)} %convert_element_type.462), channel_id=1, source_target_pairs={{16,0},{17,1},{18,2},{19,3},{20,4},{21,5},{22,6},{23,7},{24,8},{25... | collective-permute-start | bytes 4718600 | tf_op jit(solution)/shard_map/ppermute | solution.py:16
  1396.0 41.8 %copy-start.154 = (f32[512]{0:T(512)}, f32[512]{0:T(512)S(1)}, u32[]{:S(2)}) copy-start(f32[512]{0:T(512)S(1)} %get-tuple-element.1089) | copy-start | bytes 6148 | tf_op jit(solution)/shard_map/cond
  1396.0 41.8 %copy-start.178 = (f32[512]{0:T(512)}, f32[512]{0:T(512)S(1)}, u32[]{:S(2)}) copy-start(f32[512]{0:T(512)S(1)} %get-tuple-element.1088) | copy-start | bytes 6148 | tf_op jit(solution)/shard_map/cond
  1396.0 41.8 %copy-start.180 = (f32[512]{0:T(512)}, f32[512]{0:T(512)S(1)}, u32[]{:S(2)}) copy-start(f32[512]{0:T(512)S(1)} %get-tuple-element.1090) | copy-start | bytes 6148 | tf_op jit(solution)/shard_map/cond
  1397.7 40.1 %copy-start.96 = (f32[3328]{0:T(1024)}, f32[3328]{0:T(1024)S(1)}, u32[]{:S(2)}) copy-start(f32[3328]{0:T(1024)S(1)} %get-tuple-element.907) | copy-start | bytes 39940 | tf_op jit(solution)/shard_map/cond
  1397.7 40.1 %copy-start.102 = (f32[3328]{0:T(1024)}, f32[3328]{0:T(1024)S(1)}, u32[]{:S(2)}) copy-start(f32[3328]{0:T(1024)S(1)} %get-tuple-element.910) | copy-start | bytes 39940 | tf_op jit(solution)/shard_map/cond
  1397.7 40.1 %copy-start.108 = (f32[3328]{0:T(1024)}, f32[3328]{0:T(1024)S(1)}, u32[]{:S(2)}) copy-start(f32[3328]{0:T(1024)S(1)} %get-tuple-element.909) | copy-start | bytes 39940 | tf_op jit(solution)/shard_map/cond
  1397.8 40.1 %copy-start.114 = (f32[3328]{0:T(1024)}, f32[3328]{0:T(1024)S(1)}, u32[]{:S(2)}) copy-start(f32[3328]{0:T(1024)S(1)} %get-tuple-element.908) | copy-start | bytes 39940 | tf_op jit(solution)/shard_map/cond
  1620.0 51.6 %slice-start.53 = ((s8[6291456]{0:T(1024)(128)(4,1)}), s8[4194304]{0:T(1024)(128)(4,1)S(1)}, s32[]{:S(2)}) async-start(s8[6291456]{0:T(1024)(128)(4,1)} %bitcast.796), calls=%async_computation.62 | async-start | bytes 8388608 | tf_op jit(solution)/shard_map/cond
  1620.0 57.6 %slice-start.45 = ((s8[6291456]{0:T(1024)(128)(4,1)}), s8[4194304]{0:T(1024)(128)(4,1)S(1)}, s32[]{:S(2)}) async-start(s8[6291456]{0:T(1024)(128)(4,1)} %bitcast.785), calls=%async_computation.54 | async-start | bytes 8388608 | tf_op jit(solution)/shard_map/cond
  1632.7 44.9 %slice-start.46 = ((s8[6291456]{0:T(1024)(128)(4,1)}), s8[2097152]{0:T(1024)(128)(4,1)S(1)}, s32[]{:S(2)}) async-start(s8[6291456]{0:T(1024)(128)(4,1)} %bitcast.785), calls=%async_computation.55 | async-start | bytes 4194304 | tf_op jit(solution)/shard_map/cond
  1883.4 44.6 %copy-start.150 = (f32[1536]{0:T(1024)}, f32[1536]{0:T(1024)S(1)}, u32[]{:S(2)}) copy-start(f32[1536]{0:T(1024)S(1)} %get-tuple-element.693) | copy-start | bytes 18436
  1883.4 44.6 %copy-start.207 = (f32[48]{0:T(128)}, f32[48]{0:T(128)S(1)}, u32[]{:S(2)}) copy-start(f32[48]{0:T(128)S(1)} %get-tuple-element.687) | copy-start | bytes 580
  1883.4 44.6 %copy-start.209 = (f32[48]{0:T(128)}, f32[48]{0:T(128)S(1)}, u32[]{:S(2)}) copy-start(f32[48]{0:T(128)S(1)} %get-tuple-element.684) | copy-start | bytes 580
  1883.4 44.6 %copy-start.5 = (f32[1,3328,4]{2,0,1:T(1,128)S(1)}, f32[1,3328,4]{2,0,1:T(1,128)}, u32[]{:S(2)}) copy-start(f32[1,3328,4]{2,0,1:T(1,128)} %copy-done.3) | copy-start | bytes 159748
  1883.5 44.6 %copy-start.16 = (pred[512,1536]{1,0:T(8,128)(4,1)S(1)}, pred[512,1536]{1,0:T(8,128)(4,1)}, u32[]{:S(2)}) copy-start(pred[512,1536]{1,0:T(8,128)(4,1)} %copy-done.14) | copy-start | bytes 2359300
  1883.5 44.6 %copy-start.71 = (f32[3328]{0:T(1024)S(1)}, f32[3328]{0:T(1024)}, u32[]{:S(2)}) copy-start(f32[3328]{0:T(1024)} %copy-done.69) | copy-start | bytes 39940
  1883.5 44.6 %copy-start.74 = (s32[2,512]{1,0:T(2,128)S(1)}, s32[2,512]{1,0:T(2,128)}, u32[]{:S(2)}) copy-start(s32[2,512]{1,0:T(2,128)} %param.27) | copy-start | bytes 12292
  1883.5 44.6 %copy-start.219 = (f32[48]{0:T(128)S(1)}, f32[48]{0:T(128)}, u32[]{:S(2)}) copy-start(f32[48]{0:T(128)} %copy-done.214) | copy-start | bytes 580
  1886.9 37.6 %collective-permute-start.3 = (bf16[512,1536]{1,0:T(8,128)(2,1)}, bf16[512,1536]{1,0:T(8,128)(2,1)}, u32[]{:S(2)}, u32[]{:S(2)}) collective-permute-start(bf16[512,1536]{1,0:T(8,128)(2,1)} %convert_element_type.465), channel_id=1, source_target_pairs={{16,0},{17,1},{18,2},{19,3},{20,4},{21,5},{22,6},{23,7},{24,8},{25... | collective-permute-start | bytes 4718600 | tf_op jit(solution)/shard_map/ppermute | solution.py:16
  1943.8 41.6 %copy-start.156 = (f32[512]{0:T(512)}, f32[512]{0:T(512)S(1)}, u32[]{:S(2)}) copy-start(f32[512]{0:T(512)S(1)} %get-tuple-element.1109) | copy-start | bytes 6148 | tf_op jit(solution)/shard_map/cond
  1943.8 41.6 %copy-start.182 = (f32[512]{0:T(512)}, f32[512]{0:T(512)S(1)}, u32[]{:S(2)}) copy-start(f32[512]{0:T(512)S(1)} %get-tuple-element.1108) | copy-start | bytes 6148 | tf_op jit(solution)/shard_map/cond
  1943.8 41.6 %copy-start.184 = (f32[512]{0:T(512)}, f32[512]{0:T(512)S(1)}, u32[]{:S(2)}) copy-start(f32[512]{0:T(512)S(1)} %get-tuple-element.1110) | copy-start | bytes 6148 | tf_op jit(solution)/shard_map/cond
  1945.5 39.8 %copy-start.98 = (f32[3328]{0:T(1024)}, f32[3328]{0:T(1024)S(1)}, u32[]{:S(2)}) copy-start(f32[3328]{0:T(1024)S(1)} %get-tuple-element.920) | copy-start | bytes 39940 | tf_op jit(solution)/shard_map/cond
  2167.3 51.7 %slice-start.55 = ((s8[6291456]{0:T(1024)(128)(4,1)}), s8[4194304]{0:T(1024)(128)(4,1)S(1)}, s32[]{:S(2)}) async-start(s8[6291456]{0:T(1024)(128)(4,1)} %bitcast.800), calls=%async_computation.64 | async-start | bytes 8388608 | tf_op jit(solution)/shard_map/cond
  2167.3 57.7 %slice-start.49 = ((s8[6291456]{0:T(1024)(128)(4,1)}), s8[4194304]{0:T(1024)(128)(4,1)S(1)}, s32[]{:S(2)}) async-start(s8[6291456]{0:T(1024)(128)(4,1)} %bitcast.789), calls=%async_computation.58 | async-start | bytes 8388608 | tf_op jit(solution)/shard_map/cond
  2180.0 45.0 %slice-start.50 = ((s8[6291456]{0:T(1024)(128)(4,1)}), s8[2097152]{0:T(1024)(128)(4,1)S(1)}, s32[]{:S(2)}) async-start(s8[6291456]{0:T(1024)(128)(4,1)} %bitcast.789), calls=%async_computation.59 | async-start | bytes 4194304 | tf_op jit(solution)/shard_map/cond
  2500.5 225.2 %reduce-scatter.8.cloned.1.call-start = ((), (), s32[]{:S(2)}) async-start(), calls=%async_computation.5 | async-start | bytes 11796480 | tf_op jit(solution)/shard_map/reduce_scatter | solution.py:262
  2532.1 236.9 %reduce-scatter.12.cloned.1.call-start = ((), (), s32[]{:S(2)}) async-start(), calls=%async_computation.7 | async-start | bytes 1064960
  2534.4 194.0 %copy-start.33 = (f32[1,512,1536]{2,1,0:T(8,128)S(1)}, f32[1,512,1536]{2,1,0:T(8,128)}, u32[]{:S(2)}) copy-start(f32[1,512,1536]{2,1,0:T(8,128)} %get-tuple-element.1122) | copy-start | bytes 9437188
  2534.4 477.0 %all-reduce.103.cloned.1.call-start = ((), (), s32[]{:S(2)}) async-start(), calls=%async_computation.8 | async-start | bytes 14622720 | tf_op jit(solution)/shard_map/psum | solution.py:288
  (184 other events, 2331.8 us)
Sparse Core Ops, SparseCore 0:
  9.5 76.5 all-gather.4
  88.3 126.5 all-gather.2
  2500.6 144.1 reduce-scatter.9
  2647.8 77.8 reduce-scatter.7
  2728.1 23.6 reduce-scatter.11
  2754.1 257.2 all-reduce.102
where the time goes:
time: 3040 us; the launch traced here: 3030 us
  waiting for transfers between devices  1250 us (41%)
  local copies, waits for them, and re-layouts  574 us (19%)
  matrix products  560 us (18%)
  other arithmetic  532 us (18%)
  blocking collectives  77.6 us (3%)
    ppermute x4, waiting for transfers between devices, shifted_2(): lax.ppermute(value, axis, [(source, source + steps) for source in range(i...  707 us
    dot_general x8, matrix products, block_scan(): jnp.einsum('bhts,bshp->bthp', decays * scores[:, None], values, precision...  238 us
    psum x1, waiting for transfers between devices, per_device(): lax.psum(totals[0].astype(jnp.bfloat16), 'rep').astype(jnp.float32)  214 us
    all_gather x1, waiting for transfers between devices, per_device(): lax.all_gather(in_weight, 'fsdp', axis=1, tiled=True)  129 us
    unnamed x8, waiting for transfers between devices  111 us
    dynamic_update_slice x12, other arithmetic, store_slot(): lax.dynamic_update_index_in_dim(buffer, jnp.where(active, update, previou...  73.7 us
    reduce_scatter x1, waiting for transfers between devices, per_device(): lax.psum_scatter(totals[1].astype(jnp.bfloat16), 'fsdp', scatter_dimensio...  73.4 us
    slice x12, local copies, waits for them, and re-layouts, mixer(): shifted = jnp.pad(conv_in[:length - offset], ((offset, 0), (0, 0)))  67.7 us
  transfers between devices with their start and end apart: 10, of which 8 were waited for; matrix products, arithmetic and copies ran while one was open for 5% of the time, Pallas kernels for 0%

commit v1 on v0

v1 whole, which is shorter than its diff:
```python
import jax
import jax.numpy as jnp
from jax import lax
from jax.experimental import pallas as pl
from jax.experimental.pallas import tpu as pltpu
from jax.sharding import PartitionSpec as P

HIGHEST = lax.Precision.HIGHEST
EPS = 1e-05
SB = 128
REACH = 2
HG = 4
HW = 64
GW = HG * HW
LOG2E = 1.4426950408889634


def dotf(a, b, precision=None):
    return lax.dot_general(a, b, (((1,), (0,)), ((), ())), precision=precision,
                           preferred_element_type=jnp.float32)


def dot_nt(a, b, precision=None):
    return lax.dot_general(a, b, (((1,), (1,)), ((), ())), precision=precision,
                           preferred_element_type=jnp.float32)


def dot_tn(a, b, precision=None):
    return lax.dot_general(a, b, (((0,), (0,)), ((), ())), precision=precision,
                           preferred_element_type=jnp.float32)


def sigmoid(v):
    return 0.5 * jnp.tanh(0.5 * v) + 0.5


def conv(v, cp, tok):
    out = cp[4:5] + cp[3:4] * v
    for o in range(1, 4):
        out = out + cp[3 - o:4 - o] * (pltpu.roll(v, o, 0) * tok[:, o:o + 1])
    return out


def conv_back(v, dout, cp, tok):
    length = v.shape[0]
    dv = cp[3:4] * dout
    taps = [None] * 4
    taps[3] = jnp.sum(dout * v, 0, keepdims=True)
    for o in range(1, 4):
        m = dout * tok[:, o:o + 1]
        dv = dv + cp[3 - o:4 - o] * pltpu.roll(m, length - o, 0)
        taps[3 - o] = jnp.sum(m * pltpu.roll(v, o, 0), 0, keepdims=True)
    return dv, taps, jnp.sum(dout, 0, keepdims=True)


def head_spread(g, transposed):
    shape = (GW, 128) if transposed else (128, GW)
    lane = lax.broadcasted_iota(jnp.int32, shape, 0 if transposed else 1)
    head = lax.broadcasted_iota(jnp.int32, shape, 1 if transposed else 0)
    first = lane - (head - HG * g) * HW
    return ((first >= 0) & (first < HW)).astype(jnp.float32)


def softplus(v):
    return jnp.maximum(v, 0.0) + jnp.log1p(jnp.exp(-jnp.abs(v)))


def prepare(tail_ref, tok, hp_ref, step_scr, cumg_scr, cumt_scr, groups):
    length = tok.shape[0]
    row = lax.broadcasted_iota(jnp.int32, (length, 128), 0)
    raw = tail_ref[0, :, 256:384] + hp_ref[0:1, :]
    step = softplus(raw)
    total = step * hp_ref[1:2, :]
    k = 1
    while k < length:
        total = total + jnp.where(row >= k, pltpu.roll(total, k, 0), 0.0)
        k *= 2
    total = total * LOG2E
    step_scr[...] = step
    cumt_scr[...] = total.T
    for g in range(groups):
        cumg_scr[g] = pltpu.roll(total, (128 - HG * g) % 128, 1)


def pair_mask(i, j, tok, docrow, swap):
    ids = tok[(j if swap else i) * SB:((j if swap else i) + 1) * SB, 0:1]
    other = docrow[:, (i if swap else j) * SB:((i if swap else j) + 1) * SB]
    same = ids == other
    if i == j:
        r = lax.broadcasted_iota(jnp.int32, (SB, SB), 0)
        c = lax.broadcasted_iota(jnp.int32, (SB, SB), 1)
        same = same & ((c >= r) if swap else (c <= r))
    return same


def fwd_kernel(main_ref, tail_ref, tok_ref, doc_ref, cpx_ref, cpt_ref, hp_ref,
               gg_ref, ysc_ref, ss_ref, msc_scr, step_scr, cumg_scr, cumt_scr):
    g = pl.program_id(1)
    length = tok_ref.shape[1]
    blocks = length // SB
    groups = cumg_scr.shape[0]
    tok = tok_ref[0]

    @pl.when(g == 0)
    def _():
        prepare(tail_ref, tok, hp_ref, step_scr, cumg_scr, cumt_scr, groups)
        cpt = cpt_ref[...]
        bc = conv(tail_ref[0, :, :256], cpt, tok)
        bc = bc * sigmoid(bc)
        bmat, cmat = bc[:, :128], bc[:, 128:]
        docrow = doc_ref[0]
        for i in range(blocks):
            j0 = max(0, i - REACH)
            for j in range(j0, i + 1):
                sc = dot_nt(cmat[i * SB:(i + 1) * SB], bmat[j * SB:(j + 1) * SB], HIGHEST)
                msc_scr[i, :, (j - j0) * SB:(j - j0 + 1) * SB] = jnp.where(
                    pair_mask(i, j, tok, docrow, False), sc, 0.0)

    cp = cpx_ref[...]
    v = conv(main_ref[0, :, GW:], cp, tok)
    xa = v * sigmoid(v)
    stepw = dotf(step_scr[...], head_spread(g, False), HIGHEST)
    xt = (xa * stepw).astype(jnp.bfloat16)
    cumc = cumg_scr[g]
    low_half = lax.broadcasted_iota(jnp.int32, (SB, 128), 1) < HW
    for p in range(HG // 2):
        lanes = slice(p * 128, (p + 1) * 128)
        xp = xt[:, lanes]
        rows = [cumt_scr[pl.ds(HG * g + 2 * p + hh, 1), :] for hh in range(2)]
        for i in range(blocks):
            j0 = max(0, i - REACH)
            width = (i + 1 - j0) * SB
            ts = slice(i * SB, (i + 1) * SB)
            qs = slice(j0 * SB, (i + 1) * SB)
            parts = []
            for hh in range(2):
                col = cumc[ts, 2 * p + hh:2 * p + hh + 1]
                decay = jnp.exp2(jnp.minimum(col - rows[hh][:, qs], 0.0))
                w = (decay * msc_scr[i, :, :width]).astype(jnp.bfloat16)
                parts.append(dotf(w, xp[qs]))
            ysc_ref[0, ts, lanes] = jnp.where(low_half, parts[0], parts[1])
    z = main_ref[0, :, :GW]
    gated = (ysc_ref[0] + cp[6:7] * xa) * (z * sigmoid(z))
    gg_ref[0] = (gated * cp[5:6]).astype(jnp.bfloat16)
    sq = gated * gated
    sq = sq[:, :128] + sq[:, 128:]

    @pl.when(g == 0)
    def _():
        ss_ref[0] = sq

    @pl.when(g > 0)
    def _():
        ss_ref[0] = ss_ref[0] + sq


def mixer_forward(proj, tok, docrow, cp, hp):
    seqs, length, width = proj.shape
    groups = width // (2 * GW) - 1
    blocks = length // SB
    cost = pl.CostEstimate(flops=seqs * groups * HG * length * 400 * 128 * 2,
                           transcendentals=seqs * groups * HG * length * 400,
                           bytes_accessed=seqs * length * (width * 4 + groups * GW * 6))
    return pl.pallas_call(
        fwd_kernel,
        grid=(seqs, groups),
        in_specs=[
            pl.BlockSpec((1, length, 2 * GW), lambda s, g: (s, 0, g)),
            pl.BlockSpec((1, length, 2 * GW), lambda s, g: (s, 0, groups)),
            pl.BlockSpec((1, length, 8), lambda s, g: (s, 0, 0)),
            pl.BlockSpec((1, 1, length), lambda s, g: (s, 0, 0)),
            pl.BlockSpec((8, GW), lambda s, g: (0, g)),
            pl.BlockSpec((8, GW), lambda s, g: (0, groups)),
            pl.BlockSpec((8, 128), lambda s, g: (0, 0)),
        ],
        out_specs=[
            pl.BlockSpec((1, length, GW), lambda s, g: (s, 0, g)),
            pl.BlockSpec((1, length, GW), lambda s, g: (s, 0, g)),
            pl.BlockSpec((1, length, 128), lambda s, g: (s, 0, 0)),
        ],
        out_shape=[
            jax.ShapeDtypeStruct((seqs, length, groups * GW), jnp.bfloat16),
            jax.ShapeDtypeStruct((seqs, length, groups * GW), jnp.float32),
            jax.ShapeDtypeStruct((seqs, length, 128), jnp.float32),
        ],
        scratch_shapes=[
            pltpu.VMEM((blocks, SB, (REACH + 1) * SB), jnp.float32),
            pltpu.VMEM((length, 128), jnp.float32),
            pltpu.VMEM((groups, length, 128), jnp.float32),
            pltpu.VMEM((128, length), jnp.float32),
        ],
        compiler_params=pltpu.CompilerParams(
            dimension_semantics=("arbitrary", "arbitrary"), vmem_limit_bytes=48 << 20),
        cost_estimate=cost,
        name="mixer_forward",
    )(proj, proj, tok, docrow, cp, cp, hp)


def bwd_kernel(main_ref, tail_ref, ysc_ref, dm_ref, coef_ref, tok_ref, doc_ref, cpx_ref,
               cpt_ref, hp_ref, dproj_ref, col_ref, head_ref,
               msc_scr, step_scr, cumg_scr, cumt_scr, bc_scr, dsc_scr, dxt_scr, dcum_scr,
               dstep_scr):
    g = pl.program_id(1)
    length = tok_ref.shape[1]
    blocks = length // SB
    groups = cumg_scr.shape[0]
    tok = tok_ref[0]

    @pl.when(g == 0)
    def _():
        prepare(tail_ref, tok, hp_ref, step_scr, cumg_scr, cumt_scr, groups)
        cpt = cpt_ref[...]
        bc = conv(tail_ref[0, :, :256], cpt, tok)
        bc = bc * sigmoid(bc)
        bc_scr[...] = bc.astype(jnp.bfloat16)
        bmat, cmat = bc[:, :128], bc[:, 128:]
        docrow = doc_ref[0]
        for j in range(blocks):
            for i in range(j, min(blocks, j + REACH + 1)):
                sc = dot_nt(bmat[j * SB:(j + 1) * SB], cmat[i * SB:(i + 1) * SB], HIGHEST)
                msc_scr[j, :, (i - j) * SB:(i - j + 1) * SB] = jnp.where(
                    pair_mask(i, j, tok, docrow, True), sc, 0.0)
        dsc_scr[...] = jnp.zeros_like(dsc_scr)
        dcum_scr[...] = jnp.zeros_like(dcum_scr)
        dstep_scr[...] = jnp.zeros_like(dstep_scr)
        head_ref[0] = jnp.zeros_like(head_ref[0])

    @pl.when(g < groups)
    def _():
        cp = cpx_ref[...]
        vin = main_ref[0, :, GW:]
        v = conv(vin, cp, tok)
        sg = sigmoid(v)
        xa = v * sg
        dsilu_v = sg + xa * (1.0 - sg)
        z = main_ref[0, :, :GW]
        sz = sigmoid(z)
        silu_z = z * sz
        ysc = ysc_ref[0]
        y = ysc + cp[6:7] * xa
        gated = y * silu_z
        dm = dm_ref[0].astype(jnp.float32)
        col_ref[0, 5:6] = jnp.sum(dm * gated, 0, keepdims=True)
        dgated = dm * cp[5:6] - gated * coef_ref[0, :, 0:1]
        dy = dgated * silu_z
        dz = dgated * y * (sz + silu_z * (1.0 - sz))
        dproj_ref[0, :, :GW] = dz.astype(jnp.bfloat16)
        col_ref[0, 6:7] = jnp.sum(dy * xa, 0, keepdims=True)
        stepw = dotf(step_scr[...], head_spread(g, False), HIGHEST)
        xtb = (xa * stepw).astype(jnp.bfloat16)
        dyb = dy.astype(jnp.bfloat16)
        cumc = cumg_scr[g]
        low_half = lax.broadcasted_iota(jnp.int32, (SB, 128), 1) < HW
        zero = jnp.zeros((SB, 128), jnp.bfloat16)
        for p in range(HG // 2):
            lanes = slice(p * 128, (p + 1) * 128)
            dyp = dyb[:, lanes]
            rows = [cumt_scr[pl.ds(HG * g + 2 * p + hh, 1), :] for hh in range(2)]
            for j in range(blocks):
                i1 = min(blocks, j + REACH + 1)
                width = (i1 - j) * SB
                qs = slice(j * SB, (j + 1) * SB)
                ts = slice(j * SB, i1 * SB)
                xq = xtb[qs, lanes]
                parts = []
                acc = dsc_scr[j, :, :width]
                for hh in range(2):
                    col = cumc[qs, 2 * p + hh:2 * p + hh + 1]
                    decay = jnp.exp2(jnp.minimum(rows[hh][:, ts] - col, 0.0))
                    w = (decay * msc_scr[j, :, :width]).astype(jnp.bfloat16)
                    parts.append(dotf(w, dyp[ts]))
                    xm = jnp.where(low_half, xq, zero) if hh == 0 else jnp.where(low_half, zero, xq)
                    acc = acc + dot_nt(xm, dyp[ts]) * decay
                dsc_scr[j, :, :width] = acc
                dxt_scr[qs, lanes] = jnp.where(low_half, parts[0], parts[1])
        dxt = dxt_scr[...]
        gather = head_spread(g, True)
        dcum_scr[...] += dotf(dyb.astype(jnp.float32) * ysc - xtb.astype(jnp.float32) * dxt,
                              gather, HIGHEST)
        dstep_scr[...] += dotf(dxt * xa, gather, HIGHEST)
        dxa = dxt * stepw + cp[6:7] * dy
        dvin, taps, bias = conv_back(vin, dxa * dsilu_v, cp, tok)
        dproj_ref[0, :, GW:] = dvin.astype(jnp.bfloat16)
        for k in range(4):
            col_ref[0, k:k + 1] = taps[k]
        col_ref[0, 4:5] = bias
        col_ref[0, 7:8] = jnp.zeros_like(bias)

    @pl.when(g == groups)
    def _():
        cpt = cpt_ref[...]
        docrow = doc_ref[0]
        vin = tail_ref[0, :, :256]
        v = conv(vin, cpt, tok)
        sg = sigmoid(v)
        dsilu_v = sg + v * sg * (1.0 - sg)
        db = [None] * blocks
        dc = [None] * blocks
        for j in range(blocks):
            for i in range(j, min(blocks, j + REACH + 1)):
                ds = jnp.where(pair_mask(i, j, tok, docrow, True),
                               dsc_scr[j, :, (i - j) * SB:(i - j + 1) * SB], 0.0).astype(jnp.bfloat16)
                tb = dotf(ds, bc_scr[i * SB:(i + 1) * SB, 128:])
                tc = dot_tn(ds, bc_scr[j * SB:(j + 1) * SB, :128])
                db[j] = tb if db[j] is None else db[j] + tb
                dc[i] = tc if dc[i] is None else dc[i] + tc
        for i in range(blocks):
            dxt_scr[i * SB:(i + 1) * SB, :128] = db[i]
            dxt_scr[i * SB:(i + 1) * SB, 128:] = dc[i]
        dvin, taps, bias = conv_back(vin, dxt_scr[...] * dsilu_v, cpt, tok)
        dproj_ref[0, :, :256] = dvin.astype(jnp.bfloat16)
        for k in range(4):
            col_ref[0, k:k + 1] = taps[k]
        col_ref[0, 4:5] = bias
        col_ref[0, 5:8] = jnp.zeros((3, 256), jnp.float32)
        dlog = dcum_scr[...]
        ids = jnp.broadcast_to(tok[:, 0:1], (length, 128))
        row = lax.broadcasted_iota(jnp.int32, (length, 128), 0)
        k = 1
        while k < length:
            same = (pltpu.roll(ids, length - k, 0) == ids) & (row < length - k)
            dlog = dlog + jnp.where(same, pltpu.roll(dlog, length - k, 0), 0.0)
            k *= 2
        raw = tail_ref[0, :, 256:384] + hp_ref[0:1, :]
        rate = hp_ref[1:2, :]
        dstep = dstep_scr[...] + dlog * rate
        draw = dstep * jax.nn.sigmoid(raw)
        dproj_ref[0, :, 256:384] = draw.astype(jnp.bfloat16)
        dproj_ref[0, :, 384:] = jnp.zeros((length, 128), jnp.bfloat16)
        head_ref[0, 0:1] = jnp.sum(draw, 0, keepdims=True)
        head_ref[0, 1:2] = jnp.sum(dlog * rate * step_scr[...], 0, keepdims=True)


def mixer_backward(proj, ysc, dm, coef, tok, docrow, cp, hp):
    seqs, length, width = proj.shape
    groups = width // (2 * GW) - 1
    blocks = length // SB
    last = groups - 1
    cost = pl.CostEstimate(flops=seqs * groups * HG * length * 800 * 128 * 2,
                           transcendentals=seqs * groups * HG * length * 400,
                           bytes_accessed=seqs * length * (width * 6 + groups * GW * 8))
    return pl.pallas_call(
        bwd_kernel,
        grid=(seqs, groups + 1),
        in_specs=[
            pl.BlockSpec((1, length, 2 * GW), lambda s, g: (s, 0, jnp.minimum(g, last))),
            pl.BlockSpec((1, length, 2 * GW), lambda s, g: (s, 0, groups)),
            pl.BlockSpec((1, length, GW), lambda s, g: (s, 0, jnp.minimum(g, last))),
            pl.BlockSpec((1, length, GW), lambda s, g: (s, 0, jnp.minimum(g, last))),
            pl.BlockSpec((1, length, 8), lambda s, g: (s, 0, 0)),
            pl.BlockSpec((1, length, 8), lambda s, g: (s, 0, 0)),
            pl.BlockSpec((1, 1, length), lambda s, g: (s, 0, 0)),
            pl.BlockSpec((8, GW), lambda s, g: (0, jnp.minimum(g, last))),
            pl.BlockSpec((8, GW), lambda s, g: (0, groups)),
            pl.BlockSpec((8, 128), lambda s, g: (0, 0)),
        ],
        out_specs=[
            pl.BlockSpec((1, length, 2 * GW), lambda s, g: (s, 0, g)),
            pl.BlockSpec((1, 8, GW), lambda s, g: (s, 0, g)),
            pl.BlockSpec((1, 8, 128), lambda s, g: (s, 0, 0)),
        ],
        out_shape=[
            jax.ShapeDtypeStruct((seqs, length, width), jnp.bfloat16),
            jax.ShapeDtypeStruct((seqs, 8, (groups + 1) * GW), jnp.float32),
            jax.ShapeDtypeStruct((seqs, 8, 128), jnp.float32),
        ],
        scratch_shapes=[
            pltpu.VMEM((blocks, SB, (REACH + 1) * SB), jnp.float32),
            pltpu.VMEM((length, 128), jnp.float32),
            pltpu.VMEM((groups, length, 128), jnp.float32),
            pltpu.VMEM((128, length), jnp.float32),
            pltpu.VMEM((length, 256), jnp.bfloat16),
            pltpu.VMEM((blocks, SB, (REACH + 1) * SB), jnp.float32),
            pltpu.VMEM((length, GW), jnp.float32),
            pltpu.VMEM((length, 128), jnp.float32),
            pltpu.VMEM((length, 128), jnp.float32),
        ],
        compiler_params=pltpu.CompilerParams(
            dimension_semantics=("arbitrary", "arbitrary"), vmem_limit_bytes=56 << 20),
        cost_estimate=cost,
        name="mixer_backward",
    )(proj, proj, ysc, dm, coef, tok, docrow, cp, cp, hp)


def prenorm(hidden, gain):
    return hidden * lax.rsqrt(jnp.mean(hidden * hidden, -1, keepdims=True) + EPS) * gain


def prenorm_back(hidden, gain, dnorm):
    inv = lax.rsqrt(jnp.mean(hidden * hidden, -1, keepdims=True) + EPS)
    scaled = hidden * inv
    dgain = jnp.sum(dnorm * scaled, 0)
    dn = dnorm * gain
    return inv * (dn - scaled * jnp.mean(dn * scaled, -1, keepdims=True)), dgain


def head_lists(heads, shards):
    per = heads // shards
    if per % 2 == 0:
        return [[f * per + x * (per // 2) + i for f in range(shards) for i in range(per // 2)]
                for x in range(2)]
    return [list(range(x * (heads // 2), (x + 1) * (heads // 2))) for x in range(2)]


def runs(items):
    out = []
    for item in items:
        if out and out[-1][1] == item:
            out[-1][1] = item + 1
        else:
            out.append([item, item + 1])
    return out


def take(value, items, width, base, axis):
    return [lax.slice_in_dim(value, base + a * width, base + b * width, axis=axis)
            for a, b in runs(items)]


def pick(x, first, second):
    return jnp.where(x == 0, first, second)


def local_columns(weight, heads, inner, state):
    pieces = []
    for g in range(len(heads) // HG):
        mine = heads[g * HG:(g + 1) * HG]
        pieces += take(weight, mine, HW, 0, 1) + take(weight, mine, HW, inner, 1)
    pieces.append(weight[:, 2 * inner:2 * inner + 2 * state])
    pieces += take(weight, heads, 1, 2 * inner + 2 * state, 1)
    pad = 2 * GW - 2 * state - len(heads)
    pieces.append(jnp.zeros((weight.shape[0], pad), weight.dtype))
    return jnp.concatenate(pieces, 1)


def canonical_columns(parts, lists, inner, state):
    where = {h: (x, k) for x in range(2) for k, h in enumerate(lists[x])}
    heads = len(where)

    def column(h, kind):
        x, k = where[h]
        return x, (k // HG) * 2 * GW + kind * GW + (k % HG) * HW, HW

    def collect(spans):
        merged = []
        for x, start, size in spans:
            if merged and merged[-1][0] == x and merged[-1][2] == start:
                merged[-1][2] = start + size
            else:
                merged.append([x, start, start + size])
        return [parts[x][:, a:b] for x, a, b in merged]

    tail = (len(lists[0]) // HG) * 2 * GW
    pieces = collect([column(h, 0) for h in range(heads)])
    pieces += collect([column(h, 1) for h in range(heads)])
    both = slice(tail, tail + 2 * state)
    pieces.append(parts[0][:, both] + parts[1][:, both])
    pieces += collect([(where[h][0], tail + 2 * state + where[h][1], 1) for h in range(heads)])
    return jnp.concatenate(pieces, 1)


def per_device(inputs, cotangent, doc_ids, in_weight, out_weight, conv_weight, conv_bias,
               step_bias, decay_log, skip_gain, pre_gain, mix_gain):
    x = lax.axis_index("section")
    shards = lax.axis_size("fsdp")
    shard = lax.axis_index("fsdp")
    seqs, length, width = inputs.shape
    inner = mix_gain.shape[1] * shards
    heads = decay_log.shape[1] * shards
    taps = conv_weight.shape[2]
    channels = conv_bias.shape[1] * shards
    state = (channels - inner) // 2
    lists = head_lists(heads, shards)
    even = (heads // shards) % 2 == 0
    half = inner // 2
    swap = [(0, 1), (1, 0)]

    def across(value):
        return lax.ppermute(value, "section", swap)

    small = [conv_weight[0].reshape(-1), conv_bias[0], step_bias[0], decay_log[0], skip_gain[0],
             pre_gain[0], mix_gain[0]]
    sizes = [v.shape[0] for v in small]
    flat = lax.all_gather(jnp.concatenate(small), ("section", "fsdp"), axis=0)
    flat = flat.astype(jnp.float32).reshape(2, shards, -1)
    small_parts = []
    start = 0
    for size in sizes:
        small_parts.append(flat[:, :, start:start + size])
        start += size
    conv_w = small_parts[0].reshape(2, channels, taps)
    conv_b, step_b, decay, skip, pre, mix = [v.reshape(2, -1) for v in small_parts[1:]]

    def local_rows(values, fill):
        return pick(x, *[jnp.concatenate(take(values, lists[k], fill, 0, 1), 1) for k in range(2)])

    def chans(values):
        return jnp.concatenate([local_rows(values[:, :inner], HW), values[:, inner:]], 1)

    cps, hps = [], []
    taps_local = [chans(conv_w[:, :, k]) for k in range(taps)]
    bias_local = chans(conv_b)
    wide = lambda v: jnp.pad(v, ((0, 0), (0, 2 * state)))
    mix_local = wide(local_rows(mix, HW))
    skip_local = wide(jnp.repeat(local_rows(skip, 1), HW, axis=1))
    step_local = jnp.pad(local_rows(step_b, 1), ((0, 0), (0, 128 - heads // 2)))
    rate_local = jnp.pad(-jnp.exp(local_rows(decay, 1)), ((0, 0), (0, 128 - heads // 2)))
    zero_row = jnp.zeros_like(bias_local)
    cp_all = jnp.stack(taps_local + [bias_local, mix_local, skip_local, zero_row], 1)
    hp_all = jnp.stack([step_local, rate_local] + [jnp.zeros_like(rate_local)] * 6, 1)

    in_both = [local_columns(in_weight[0], lists[k], inner, state) for k in range(2)]
    in_mine, in_other = pick(x, *in_both), pick(x, *in_both[::-1])
    in_far = across(in_other)
    in_shards = [pick(x, in_mine, in_far), pick(x, in_far, in_mine)]
    in_full = [lax.all_gather(v, "fsdp", axis=0, tiled=True) for v in in_shards]
    if even:
        per = half // shards
        out_both = [out_weight[0, :per], out_weight[0, per:]]
        out_mine, out_other = pick(x, *out_both), pick(x, *out_both[::-1])
        out_far = across(out_other)
        out_full = [lax.all_gather(v, "fsdp", axis=0, tiled=True)
                    for v in (pick(x, out_mine, out_far), pick(x, out_far, out_mine))]
    else:
        whole = lax.all_gather(out_weight[0], "fsdp", axis=0, tiled=True)
        out_both = [whole[:half], whole[half:]]
        out_mine, out_other = pick(x, *out_both), pick(x, *out_both[::-1])
        out_far = across(out_other)
        out_full = [pick(x, out_mine, out_far), pick(x, out_far, out_mine)]

    ids = doc_ids.astype(jnp.float32)
    links = [ids]
    for o in range(1, taps):
        links.append((jnp.pad(doc_ids[:, :length - o], ((0, 0), (o, 0)), constant_values=-1)
                      == doc_ids).astype(jnp.float32))
    tok = jnp.stack(links + [jnp.zeros_like(ids)] * (8 - taps), -1)
    docrow = ids[:, None]

    saved = [[None] * seqs for _ in range(2)]
    outputs = [[None] * seqs for _ in range(2)]
    hidden = [inputs[i] for i in range(seqs)]
    for s in range(2):
        for i in range(seqs):
            h = hidden[i]
            normed = prenorm(h, pre[s]).astype(jnp.bfloat16)
            proj = dotf(normed, in_full[s])
            gg, ysc, ss = mixer_forward(proj[None], tok[i:i + 1], docrow[i:i + 1], cp_all[s],
                                        hp_all[s])
            ss = jnp.sum(ss[0], -1, keepdims=True)
            part = dotf(gg[0], out_full[s]).astype(jnp.bfloat16)
            u = part.astype(jnp.float32) + across(part).astype(jnp.float32)
            r = lax.rsqrt((ss + across(ss)) / inner + EPS)
            result = h + r * u
            outputs[s][i] = result
            saved[s][i] = (h, normed, proj, gg, ysc, u, r)
            hidden[i] = result.astype(jnp.bfloat16).astype(jnp.float32)

    grads_in, grads_out, grads_small = [None] * 2, [None] * 2, [None] * 2
    in_grads = [[None] * seqs for _ in range(2)]
    upstream = [cotangent[i] for i in range(seqs)]
    for s in (1, 0):
        din, dout, dsmall = None, None, None
        for i in range(seqs):
            h, normed, proj, gg, ysc, u, r = saved[s][i]
            g = upstream[i]
            gr = (r * g).astype(jnp.bfloat16)
            dm = dot_nt(gr, out_full[s])
            coef = r * r * jnp.sum(gr.astype(jnp.float32) * u, -1, keepdims=True) / inner
            dproj, col, head = mixer_backward(
                proj[None], ysc, dm[None], jnp.pad(coef, ((0, 0), (0, 7)))[None], tok[i:i + 1],
                docrow[i:i + 1], cp_all[s], hp_all[s])
            dnp = dot_nt(dproj[0], in_full[s]).astype(jnp.bfloat16)
            dn = dnp.astype(jnp.float32) + across(dnp).astype(jnp.float32)
            dh, dpre = prenorm_back(h, pre[s], dn)
            dh = g + dh
            in_grads[s][i] = dh
            upstream[i] = dh.astype(jnp.bfloat16).astype(jnp.float32)
            t_in, t_out = dot_tn(normed, dproj[0]), dot_tn(gg[0], gr)
            t_small = jnp.concatenate([col[0].reshape(-1), head[0, :2].reshape(-1), dpre])
            if i == 0:
                din, dout, dsmall = t_in, t_out, t_small
            else:
                din, dout, dsmall = din + t_in, dout + t_out, dsmall + t_small
        grads_in[s] = lax.psum_scatter(din.astype(jnp.bfloat16), "fsdp", scatter_dimension=0,
                                       tiled=True)
        if even:
            grads_out[s] = lax.psum_scatter(dout.astype(jnp.bfloat16), "fsdp",
                                            scatter_dimension=0, tiled=True)
        else:
            grads_out[s] = dout.astype(jnp.bfloat16)
        grads_small[s] = lax.psum(dsmall, ("fsdp", "rep"))

    def arrange(pair):
        keep, send = pick(x, *pair), pick(x, *pair[::-1])
        got = across(send)
        return [pick(x, keep, got), pick(x, got, keep)], keep

    parts, _ = arrange(grads_in)
    grad_in = lax.psum(canonical_columns(parts, lists, inner, state), "rep").astype(jnp.float32)
    parts, _ = arrange(grads_out)
    grad_out = jnp.concatenate(parts, 0)
    if not even:
        grad_out = lax.psum_scatter(grad_out, "fsdp", scatter_dimension=0, tiled=True)
    grad_out = lax.psum(grad_out, "rep").astype(jnp.float32)
    parts, keep = arrange(grads_small)
    cols = half + 2 * state
    where = {h: (k, j) for k in range(2) for j, h in enumerate(lists[k])}

    def ordered(pair, size):
        pieces = []
        for a, b in runs(range(heads)):
            for h in range(a, b):
                k, j = where[h]
                pieces.append(pair[k][..., j * size:(j + 1) * size])
        return jnp.concatenate(pieces, -1)

    col_parts = [v[:8 * cols].reshape(8, cols) for v in parts]
    head_parts = [v[8 * cols:8 * cols + 256].reshape(2, 128) for v in parts]
    col_x = ordered(col_parts, HW)
    col_bc = col_parts[0][:5, half:] + col_parts[1][:5, half:]
    conv_grads = jnp.concatenate([col_x[:5], col_bc], 1)
    head_grads = ordered(head_parts, 1)

    def own(value, axis=-1):
        size = value.shape[axis] // shards
        return lax.dynamic_slice_in_dim(value, shard * size, size, axis % value.ndim)

    return (
        pick(x, jnp.stack(outputs[0]), jnp.stack(outputs[1]))[None],
        pick(x, jnp.stack(in_grads[0]), jnp.stack(in_grads[1]))[None],
        grad_in[None],
        grad_out[None],
        own(conv_grads[:4]).T[None],
        own(conv_grads[4])[None],
        own(head_grads[0])[None],
        own(head_grads[1])[None],
        own(jnp.sum(col_x[6].reshape(heads, HW), -1))[None],
        own(keep[8 * cols + 256:])[None],
        own(col_x[5])[None],
    )


def solution(mesh):
    rows = P(("fsdp", "rep"), None, None)
    return jax.shard_map(
        per_device,
        mesh=mesh,
        in_specs=(rows, rows, P(("fsdp", "rep"), None), P("section", "fsdp", None),
                  P("section", "fsdp", None), P("section", "fsdp", None)) + (P("section", "fsdp"),) * 6,
        out_specs=(P("section", ("fsdp", "rep"), None, None),) * 2
        + (P("section", "fsdp", None),) * 3 + (P("section", "fsdp"),) * 6,
        check_vma=False,
    )
```

time: 3040 us -> 1290 us (0.42)
  waiting for transfers between devices: 1250 us -> 666 us
  local copies, waits for them, and re-layouts: 574 us -> 103 us
  other arithmetic: 532 us -> 86.2 us
  matrix products: 560 us -> 208 us
  Pallas kernels: 0 us -> 175 us
  blocking collectives: 77.6 us -> 0 us
    ppermute x4 -> x17, waiting for transfers between devices: 707 us -> 232 us  [across(): return lax.ppermute(value, 'section', swap)]
    dot_general x42 -> x24, matrix products: 550 us -> 208 us  [the longest x8 74.7 us: dot_tn(): lax.dot_general(a, b, (((0,), (0,)), ((), ())), precision=precision, pref...]
    pallas_call x0 -> x8, Pallas kernels: none -> 175 us  [the longest x4 119 us: mixer_backward(): pl.pallas_call(bwd_kernel, grid=(seqs, groups + 1), in_specs=[pl.BlockSpe...]
    reshape x26 -> x7, local copies, waits for them, and re-layouts: 172 us -> 6.9 us  [the longest x1 5.28 us: per_device(): conv_w = small_parts[0].reshape(2, channels, taps)]
    all_gather x2 -> x4, waiting for transfers between devices: 141 us -> 15.9 us  [the longest x2 11.8 us: per_device(): lax.all_gather(v, 'fsdp', axis=0, tiled=True)]
    reduce_sum x20 -> x9, other arithmetic: 140 us -> 21.7 us  [the longest x2 13.2 us: per_device(): jnp.sum(gr.astype(jnp.float32) * u, -1, keepdims=True)]
    convert_element_type x32 -> x1, other arithmetic: 111 us -> 0.01 us  [per_device(): ids = doc_ids.astype(jnp.float32)]
    unnamed x8 -> x12, waiting for transfers between devices: 111 us -> 0.71 us
  transfers between devices with their start and end apart: 10 -> 28, of which waited for: 8 -> 15; matrix products, arithmetic and copies ran while one was open for 5% -> 24% of each run, Pallas kernels for 0% -> 9%
where the time goes in v1:
time: 1290 us; the launch traced here: 1280 us
  waiting for transfers between devices  666 us (52%)
  matrix products  208 us (16%)
  Pallas kernels  175 us (14%)
  local copies, waits for them, and re-layouts  103 us (8%)
  other arithmetic  86.2 us (7%)
  starting transfers between devices  24 us (2%)
  between operations  18 us (1%)
    psum x1, waiting for transfers between devices, per_device(): lax.psum(canonical_columns(parts, lists, inner, state), 'rep')  249 us
    ppermute x17, waiting for transfers between devices, across(): return lax.ppermute(value, 'section', swap)  232 us
    pallas_call x4, Pallas kernels, mixer_backward(): pl.pallas_call(bwd_kernel, grid=(seqs, groups + 1), in_specs=[pl.BlockSpe...  119 us
    reduce_scatter x2, waiting for transfers between devices, per_device(): lax.psum_scatter(dout.astype(jnp.bfloat16), 'fsdp', scatter_dimension=0,...  96.6 us
    dot_general x8, matrix products, dot_tn(): lax.dot_general(a, b, (((0,), (0,)), ((), ())), precision=precision, pref...  74.7 us
    dot_general x8, matrix products, dotf(): lax.dot_general(a, b, (((1,), (0,)), ((), ())), precision=precision, pref...  67.4 us
    dot_general x8, matrix products, dot_nt(): lax.dot_general(a, b, (((1,), (1,)), ((), ())), precision=precision, pref...  66.1 us
    pallas_call x4, Pallas kernels, mixer_forward(): pl.pallas_call(fwd_kernel, grid=(seqs, groups), in_specs=[pl.BlockSpec((1...  55.4 us
  transfers between devices with their start and end apart: 28, of which 15 were waited for; matrix products, arithmetic and copies ran while one was open for 24% of the time, Pallas kernels for 9%

profile of v1, /device:TPU:0, one launch (start us, length us, event | category | flops | bytes accessed | tf_op | source)
XLA Modules:
  0.0 1280.0 jit_solution(2952543710701731242)
XLA Ops:
  8.1 7.5 copy.121
  41.6 58.2 %collective-permute-done = bf16[384,3584]{1,0:T(8,128)(2,1)} collective-permute-done((bf16[384,3584]{1,0:T(8,128)(2,1)}, bf16[384,3584]{1,0:T(8,128)(2,1)}, u32[]{:S(2)}, u32[]{:S(2)}) %collective-permute-start) | collective-permute-done | bytes 2752544 | tf_op jit(solution)/shard_map/ppermute | solution.py:479
  107.8 26.3 %collective-permute-done.2 = bf16[384,1536]{1,0:T(8,128)(2,1)S(1)} collective-permute-done((bf16[384,1536]{1,0:T(8,128)(2,1)S(1)}, bf16[384,1536]{1,0:T(8,128)(2,1)S(1)}, u32[]{:S(2)}, u32[]{:S(2)}) %collective-permute-start.2) | collective-permute-done | bytes 1179680 | tf_op jit(solution)/shard_map/ppermute | solution.py:479
  149.1 13.0 %fusion.116 = (f32[2,3328,1]{2,1,0:T(8,128)}, f32[2,3328,1]{2,1,0:T(8,128)}, f32[2,3328,1]{2,1,0:T(8,128)}, f32[2,3328,1]{2,1,0:T(8,128)}) fusion(f32[2,3328,4]{2,1,0:T(8,128)} %reshape.316), kind=kLoop, calls=%fused_computation.249 | loop fusion | bytes 212992 | tf_op jit(solution)/shard_map/slice | solution.py:501
  178.9 11.6 convolution_bitcast_fusion.3.main_ref.tail_ref
  190.5 13.7 %mixer_forward.4 = (bf16[1,512,1536]{2,1,0:T(8,128)(2,1)S(1)}, f32[1,512,1536]{2,1,0:T(8,128)S(1)}, f32[1,512,128]{2,1,0:T(8,128)S(1)}) custom-call(f32[1,512,3584]{2,1,0:T(8,128)} %convolution_bitcast_fusion.3.main_ref.tail_ref, f32[1,512,3584]{2,1,0:T(8,128)} %convolution_bitcast_fusion.3.main_ref.tail_ref, f32[1,512,8]{2,1,0:T(8,128)S(1)} %get-tuple-element.247.tok_ref, ...), custom_call_target="tpu_custom_call" | custom-call | flops 1258291200 | bytes 12058624 | tf_op jit(solution)/shard_map/mixer_forward/pallas_call | solution.py:164
  205.9 11.8 all-gather.8.cloned.1.call-done
  217.7 6.2 convolution_convert_fusion.3
  225.3 12.9 %convolution_bitcast_fusion.2.main_ref.tail_ref = f32[1,512,3584]{2,1,0:T(8,128)} fusion(bf16[1536,3584]{1,0:T(8,128)(2,1)} %all-gather.6.cloned.1.call-done, f32[2,512,1536]{2,1,0:T(8,128)} %param.12, f32[512]{0:T(512)S(1)} %add_rsqrt_fusion.2, f32[1536]{0:T(1024)S(1)} %mul.346), kind=kOutput, calls=%fused_computation.6 | convolution fusion | flops 5639503872 | bytes 21504000 | tf_op jit(solution)/shard_map/dot_general | solution.py:19
  238.2 13.9 %mixer_forward.5 = (bf16[1,512,1536]{2,1,0:T(8,128)(2,1)S(1)}, f32[1,512,1536]{2,1,0:T(8,128)S(1)}, f32[1,512,128]{2,1,0:T(8,128)S(1)}) custom-call(f32[1,512,3584]{2,1,0:T(8,128)} %convolution_bitcast_fusion.2.main_ref.tail_ref, f32[1,512,3584]{2,1,0:T(8,128)} %convolution_bitcast_fusion.2.main_ref.tail_ref, f32[1,512,8]{2,1,0:T(8,128)S(1)} %get-tuple-element.248.tok_ref, ...), custom_call_target="tpu_custom_call" | custom-call | flops 1258291200 | bytes 12058624 | tf_op jit(solution)/shard_map/mixer_forward/pallas_call | solution.py:164
  257.7 36.7 %collective-permute-done.1 = f32[512,1]{0,1:T(1,128)S(1)} collective-permute-done((f32[512,1]{0,1:T(1,128)S(1)}, f32[512,1]{0,1:T(1,128)S(1)}, u32[]{:S(2)}, u32[]{:S(2)}) %collective-permute-start.1) | collective-permute-done | bytes 2080 | tf_op jit(solution)/shard_map/ppermute | solution.py:479
  295.5 8.1 fusion.32
  303.6 12.7 convolution_bitcast_fusion.1.main_ref.tail_ref
  316.4 13.8 %mixer_forward.6 = (bf16[1,512,1536]{2,1,0:T(8,128)(2,1)S(1)}, f32[1,512,1536]{2,1,0:T(8,128)S(1)}, f32[1,512,128]{2,1,0:T(8,128)S(1)}) custom-call(f32[1,512,3584]{2,1,0:T(8,128)} %convolution_bitcast_fusion.1.main_ref.tail_ref, f32[1,512,3584]{2,1,0:T(8,128)} %convolution_bitcast_fusion.1.main_ref.tail_ref, f32[1,512,8]{2,1,0:T(8,128)S(1)} %get-tuple-element.247.tok_ref, ...), custom_call_target="tpu_custom_call" | custom-call | flops 1258291200 | bytes 12058624 | tf_op jit(solution)/shard_map/mixer_forward/pallas_call | solution.py:164
  331.8 6.6 convolution_convert_fusion.1
  340.7 11.0 convolution_bitcast_fusion.main_ref.tail_ref
  351.7 14.1 %mixer_forward.7 = (bf16[1,512,1536]{2,1,0:T(8,128)(2,1)S(1)}, f32[1,512,1536]{2,1,0:T(8,128)S(1)}, f32[1,512,128]{2,1,0:T(8,128)S(1)}) custom-call(f32[1,512,3584]{2,1,0:T(8,128)} %convolution_bitcast_fusion.main_ref.tail_ref, f32[1,512,3584]{2,1,0:T(8,128)} %convolution_bitcast_fusion.main_ref.tail_ref, f32[1,512,8]{2,1,0:T(8,128)S(1)} %get-tuple-element.248.tok_ref, ...), custom_call_target="tpu_custom_call" | custom-call | flops 1258291200 | bytes 12058624 | tf_op jit(solution)/shard_map/mixer_forward/pallas_call | solution.py:164
  376.3 31.5 %collective-permute-done.8 = f32[512,1]{0,1:T(1,128)S(1)} collective-permute-done((f32[512,1]{0,1:T(1,128)S(1)}, f32[512,1]{0,1:T(1,128)S(1)}, u32[]{:S(2)}, u32[]{:S(2)}) %collective-permute-start.8) | collective-permute-done | bytes 2080 | tf_op jit(solution)/shard_map/ppermute | solution.py:479
  408.2 7.7 convolution_bitcast_fusion.7.dm_ref
  415.9 7.7 convolution_bitcast_fusion.5.dm_ref
  431.1 29.9 %mixer_backward.4 = (bf16[1,512,3584]{2,1,0:T(8,128)(2,1)}, f32[1,8,1792]{2,1,0:T(8,128)}, f32[1,8,128]{2,1,0:T(8,128)}) custom-call(f32[1,512,3584]{2,1,0:T(8,128)} %convolution_bitcast_fusion.1.main_ref.tail_ref, f32[1,512,3584]{2,1,0:T(8,128)} %convolution_bitcast_fusion.1.main_ref.tail_ref, f32[1,512,1536]{2,1,0:T(8,128)} %copy-done.6, ...), custom_call_target="tpu_custom_call" | custom-call | flops 2516582400 | bytes 17301504 | tf_op jit(solution)/shard_map/mixer_backward/pallas_call | solution.py:342
  461.0 12.5 fusion.18
  473.5 29.8 %mixer_backward.6 = (bf16[1,512,3584]{2,1,0:T(8,128)(2,1)}, f32[1,8,1792]{2,1,0:T(8,128)}, f32[1,8,128]{2,1,0:T(8,128)}) custom-call(f32[1,512,3584]{2,1,0:T(8,128)} %convolution_bitcast_fusion.main_ref.tail_ref, f32[1,512,3584]{2,1,0:T(8,128)} %convolution_bitcast_fusion.main_ref.tail_ref, f32[1,512,1536]{2,1,0:T(8,128)} %copy-done.7, ...), custom_call_target="tpu_custom_call" | custom-call | flops 2516582400 | bytes 17301504 | tf_op jit(solution)/shard_map/mixer_backward/pallas_call | solution.py:342
  503.3 13.9 %add_convert_fusion = bf16[1536,3584]{1,0:T(8,128)(2,1)} fusion(f32[1536,3584]{1,0:T(8,128)} %fusion.18, bf16[1,512,3584]{2,1,0:T(8,128)(2,1)} %get-tuple-element.48, bf16[512,1536]{1,0:T(8,128)(2,1)S(1)} %copy-done.25, f32[512]{0:T(512)S(1)} %add_rsqrt_fusion, f32[1536]{0:T(1024)S(1)} %mul.362), kind=kOutput, calls=%fused_computation | convolution fusion | flops 5651300352 | bytes 38281216 | tf_op jit(solution)/shard_map/dot_general | solution.py:29
  517.3 10.1 fusion.46
  529.1 10.6 fusion.52
  540.3 24.5 %collective-permute-done.10 = bf16[512,1536]{1,0:T(8,128)(2,1)S(1)} collective-permute-done((bf16[512,1536]{1,0:T(8,128)(2,1)S(1)}, bf16[512,1536]{1,0:T(8,128)(2,1)S(1)}, u32[]{:S(2)}, u32[]{:S(2)}) %collective-permute-start.10) | collective-permute-done | bytes 1572896 | tf_op jit(solution)/shard_map/ppermute | solution.py:479
  564.8 31.3 %collective-permute-done.12 = bf16[512,1536]{1,0:T(8,128)(2,1)S(1)} collective-permute-done((bf16[512,1536]{1,0:T(8,128)(2,1)S(1)}, bf16[512,1536]{1,0:T(8,128)(2,1)S(1)}, u32[]{:S(2)}, u32[]{:S(2)}) %collective-permute-start.12) | collective-permute-done | bytes 1572896 | tf_op jit(solution)/shard_map/ppermute | solution.py:479
  598.6 7.7 multiply_reduce_fusion.6
  609.1 6.6 convolution_bitcast_fusion.6.dm_ref
  615.7 30.0 %mixer_backward.5 = (bf16[1,512,3584]{2,1,0:T(8,128)(2,1)}, f32[1,8,1792]{2,1,0:T(8,128)}, f32[1,8,128]{2,1,0:T(8,128)}) custom-call(f32[1,512,3584]{2,1,0:T(8,128)} %convolution_bitcast_fusion.3.main_ref.tail_ref, f32[1,512,3584]{2,1,0:T(8,128)} %convolution_bitcast_fusion.3.main_ref.tail_ref, f32[1,512,1536]{2,1,0:T(8,128)} %copy-done.4, ...), custom_call_target="tpu_custom_call" | custom-call | flops 2516582400 | bytes 17301504 | tf_op jit(solution)/shard_map/mixer_backward/pallas_call | solution.py:342
  645.7 6.8 convolution_bitcast_fusion.4.dm_ref
  652.5 29.7 %mixer_backward.7 = (bf16[1,512,3584]{2,1,0:T(8,128)(2,1)}, f32[1,8,1792]{2,1,0:T(8,128)}, f32[1,8,128]{2,1,0:T(8,128)}) custom-call(f32[1,512,3584]{2,1,0:T(8,128)} %convolution_bitcast_fusion.2.main_ref.tail_ref, f32[1,512,3584]{2,1,0:T(8,128)} %convolution_bitcast_fusion.2.main_ref.tail_ref, f32[1,512,1536]{2,1,0:T(8,128)} %copy-done.5, ...), custom_call_target="tpu_custom_call" | custom-call | flops 2516582400 | bytes 17301504 | tf_op jit(solution)/shard_map/mixer_backward/pallas_call | solution.py:342
  682.3 12.5 fusion.14
  694.9 14.9 %add_convert_fusion.1 = bf16[1536,3584]{1,0:T(8,128)(2,1)} fusion(f32[1536,3584]{1,0:T(8,128)} %fusion.14, bf16[1,512,3584]{2,1,0:T(8,128)(2,1)} %get-tuple-element.50, f32[2,512,1536]{2,1,0:T(8,128)} %param.12, f32[512]{0:T(512)S(1)} %copy-done.57, f32[1536]{0:T(1024)S(1)} %copy-done.49), kind=kOutput, calls=%fused_computation.1 | convolution fusion | flops 5650513920 | bytes 39854080 | tf_op jit(solution)/shard_map/dot_general | solution.py:29
  715.8 7.0 add_convert_fusion.2
  736.4 7.4 maximum_select_fusion
  743.8 9.5 fusion.49
  754.7 7.1 fusion.55
  764.5 35.4 %reduce-scatter.5.cloned.1.call-done = bf16[384,3584]{1,0:T(8,128)(2,1)} async-done(((bf16[1536,3584]{1,0:T(8,128)(2,1)}), bf16[384,3584]{1,0:T(8,128)(2,1)}) %reduce-scatter.5.cloned.1.call-update) | async-done | bytes 2752528 | tf_op jit(solution)/shard_map/reduce_scatter | solution.py:584
  804.9 45.7 %reduce-scatter.11.cloned.1.call-done = bf16[384,1536]{1,0:T(8,128)(2,1)} async-done(((bf16[1536,1536]{1,0:T(8,128)(2,1)}), bf16[384,1536]{1,0:T(8,128)(2,1)}) %reduce-scatter.11.cloned.1.call-update) | async-done | bytes 1179664 | tf_op jit(solution)/shard_map/reduce_scatter | solution.py:587
  850.7 50.8 %reduce-scatter.9.cloned.1.call-done = bf16[384,1536]{1,0:T(8,128)(2,1)} async-done(((bf16[1536,1536]{1,0:T(8,128)(2,1)}), bf16[384,1536]{1,0:T(8,128)(2,1)}) %reduce-scatter.9.cloned.1.call-update) | async-done | bytes 1179664 | tf_op jit(solution)/shard_map/reduce_scatter | solution.py:587
  912.7 19.1 %collective-permute-done.15 = bf16[384,1536]{1,0:T(8,128)(2,1)} collective-permute-done((bf16[384,1536]{1,0:T(8,128)(2,1)}, bf16[384,1536]{1,0:T(8,128)(2,1)}, u32[]{:S(2)}, u32[]{:S(2)}) %collective-permute-start.15) | collective-permute-done | bytes 1179680 | tf_op jit(solution)/shard_map/ppermute | solution.py:479
  942.9 8.9 concatenate.163
  953.7 8.9 fusion.23
  962.6 36.5 %all-reduce.20.cloned.1.call-done = (f32[16128]{0:T(1024)}, f32[16128]{0:T(1024)}) async-done(((f32[16128]{0:T(1024)}, f32[16128]{0:T(1024)}), (f32[16128]{0:T(1024)}, f32[16128]{0:T(1024)})) %all-reduce.20.cloned.1.call-update) | async-done | bytes 129040 | tf_op jit(solution)/shard_map/psum | solution.py:591
  1012.7 249.0 %all-reduce.22.cloned.1.call-done = (bf16[1,384,6448]{2,1,0:T(8,128)(2,1)}, bf16[1,768,1536]{2,1,0:T(8,128)(2,1)}) async-done(((bf16[1,384,6448]{2,1,0:T(8,128)(2,1)}, bf16[1,768,1536]{2,1,0:T(8,128)(2,1)}), (bf16[1,384,6448]{2,1,0:T(8,128)(2,1)}, bf16[1,768,1536]{2,1,0:T(8,128)(2,1)})) %all-reduce.22.cloned.1.call-update) | async-done | bytes 7311376 | tf_op jit(solution)/shard_map/psum | solution.py:599
  1261.7 7.9 copy.152
  (424 shorter events, 172.9 us)
Async XLA Ops:
  8.0 134.5 %all-reduce.18.cloned.1.call-start = ((), (), s32[]{:S(2)}) async-start(), calls=%async_computation.12 | async-start | bytes 172032
  33.8 66.0 %collective-permute-start = (bf16[384,3584]{1,0:T(8,128)(2,1)}, bf16[384,3584]{1,0:T(8,128)(2,1)}, u32[]{:S(2)}, u32[]{:S(2)}) collective-permute-start(bf16[384,3584]{1,0:T(8,128)(2,1)} %broadcast_select_fusion.6), channel_id=1, source_target_pairs={{0,16},{16,0},{1,17},{17,1},{2,18},{18,2},{3,19},{19,3},{4,20},{20... | collective-permute-start | bytes 8257544 | tf_op jit(solution)/shard_map/ppermute | solution.py:479
  41.6 137.3 %all-gather.6.cloned.1.call-start = ((), (), s32[]{:S(2)}) async-start(), calls=%async_computation.4 | async-start | bytes 13762560 | tf_op jit(solution)/shard_map/all_gather | solution.py:516
  105.2 112.4 %all-gather.8.cloned.1.call-start = ((), (), s32[]{:S(2)}) async-start(), calls=%async_computation.5 | async-start | bytes 5898240 | tf_op jit(solution)/shard_map/all_gather | solution.py:522
  107.0 27.2 %collective-permute-start.2 = (bf16[384,1536]{1,0:T(8,128)(2,1)S(1)}, bf16[384,1536]{1,0:T(8,128)(2,1)S(1)}, u32[]{:S(2)}, u32[]{:S(2)}) collective-permute-start(bf16[384,1536]{1,0:T(8,128)(2,1)S(1)} %select_bitcast_fusion), channel_id=1, source_target_pairs={{0,16},{16,0},{1,17},{17,1},{2,18},{18,2},{3,19},{19,3},{4,20},{20... | collective-permute-start | bytes 3538952 | tf_op jit(solution)/shard_map/ppermute | solution.py:479
  135.9 167.7 %all-gather.10.cloned.1.call-start = ((), (), s32[]{:S(2)}) async-start(), calls=%async_computation.6 | async-start | bytes 13762560 | tf_op jit(solution)/shard_map/all_gather | solution.py:516
  136.5 195.3 %all-gather.12.cloned.1.call-start = ((), (), s32[]{:S(2)}) async-start(), calls=%async_computation.7 | async-start | bytes 5898240 | tf_op jit(solution)/shard_map/all_gather | solution.py:522
  142.4 36.5 %copy-start.54 = (f32[512]{0:T(512)}, f32[512]{0:T(512)S(1)}, u32[]{:S(2)}) copy-start(f32[512]{0:T(512)S(1)} %add_rsqrt_fusion.3) | copy-start | bytes 6148
  142.4 82.9 %copy-start.56 = (f32[512]{0:T(512)}, f32[512]{0:T(512)S(1)}, u32[]{:S(2)}) copy-start(f32[512]{0:T(512)S(1)} %add_rsqrt_fusion.2) | copy-start | bytes 6148
  142.4 174.0 %copy-start.15 = (f32[1,1,512]{2,1,0:T(1,128)}, f32[1,1,512]{2,1,0:T(1,128)S(1)}, u32[]{:S(2)}) copy-start(f32[1,1,512]{2,1,0:T(1,128)S(1)} %get-tuple-element.310.doc_ref) | copy-start | bytes 6148
  142.4 209.3 %copy-start.14 = (f32[1,1,512]{2,1,0:T(1,128)}, f32[1,1,512]{2,1,0:T(1,128)S(1)}, u32[]{:S(2)}) copy-start(f32[1,1,512]{2,1,0:T(1,128)S(1)} %get-tuple-element.311.doc_ref) | copy-start | bytes 6148
  142.5 173.9 %copy-start.1 = (f32[1,512,8]{2,1,0:T(8,128)}, f32[1,512,8]{2,1,0:T(8,128)S(1)}, u32[]{:S(2)}) copy-start(f32[1,512,8]{2,1,0:T(8,128)S(1)} %get-tuple-element.247.tok_ref) | copy-start | bytes 49156
  142.5 209.2 %copy-start = (f32[1,512,8]{2,1,0:T(8,128)}, f32[1,512,8]{2,1,0:T(8,128)S(1)}, u32[]{:S(2)}) copy-start(f32[1,512,8]{2,1,0:T(8,128)S(1)} %get-tuple-element.248.tok_ref) | copy-start | bytes 49156
  143.8 81.4 %copy-start.48 = (f32[1536]{0:T(1024)}, f32[1536]{0:T(1024)S(1)}, u32[]{:S(2)}) copy-start(f32[1536]{0:T(1024)S(1)} %mul.346) | copy-start | bytes 18436
  174.2 64.1 %copy-start.12 = (f32[8,128]{1,0:T(8,128)}, f32[8,128]{1,0:T(8,128)S(1)}, u32[]{:S(2)}) copy-start(f32[8,128]{1,0:T(8,128)S(1)} %get-tuple-element.309.hp_ref) | copy-start | bytes 12292
  174.2 177.5 %copy-start.13 = (f32[8,128]{1,0:T(8,128)}, f32[8,128]{1,0:T(8,128)S(1)}, u32[]{:S(2)}) copy-start(f32[8,128]{1,0:T(8,128)S(1)} %get-tuple-element.308.hp_ref) | copy-start | bytes 12292
  174.2 64.0 %copy-start.2 = (f32[8,1792]{1,0:T(8,128)}, f32[8,1792]{1,0:T(8,128)S(1)}, u32[]{:S(2)}) copy-start(f32[8,1792]{1,0:T(8,128)S(1)} %get-tuple-element.255.cpx_ref.cpt_ref) | copy-start | bytes 172036
  174.2 177.5 %copy-start.3 = (f32[8,1792]{1,0:T(8,128)}, f32[8,1792]{1,0:T(8,128)S(1)}, u32[]{:S(2)}) copy-start(f32[8,1792]{1,0:T(8,128)S(1)} %get-tuple-element.254.cpx_ref.cpt_ref) | copy-start | bytes 172036
  174.2 590.3 %reduce-scatter.7.cloned.1.call-start = ((), (), s32[]{:S(2)}) async-start(), calls=%async_computation.9 | async-start | bytes 13762560 | tf_op jit(solution)/shard_map/reduce_scatter | solution.py:584
  217.7 34.5 %slice-start.10 = ((s8[4718592]{0:T(1024)(128)(4,1)}), s8[4194304]{0:T(1024)(128)(4,1)S(1)}, s32[]{:S(2)}) async-start(s8[4718592]{0:T(1024)(128)(4,1)} %bitcast.307), calls=%async_computation.25 | async-start | bytes 8388608
  223.8 71.3 %collective-permute-start.3 = (bf16[512,1536]{1,0:T(8,128)(2,1)}, bf16[512,1536]{1,0:T(8,128)(2,1)}, u32[]{:S(2)}, u32[]{:S(2)}) collective-permute-start(bf16[512,1536]{1,0:T(8,128)(2,1)} %convolution_convert_fusion.3), channel_id=1, source_target_pairs={{0,16},{16,0},{1,17},{17,1},{2,18},{18,2},{3,19},{19,3},{4,20},{20... | collective-permute-start | bytes 4718600 | tf_op jit(solution)/shard_map/ppermute | solution.py:479
  254.8 40.4 %copy-start.31 = (bf16[512,1536]{1,0:T(8,128)(2,1)}, bf16[512,1536]{1,0:T(8,128)(2,1)S(1)}, u32[]{:S(2)}) copy-start(bf16[512,1536]{1,0:T(8,128)(2,1)S(1)} %convolution_convert_fusion.2) | copy-start | bytes 4718596
  254.8 40.7 %collective-permute-start.5 = (bf16[512,1536]{1,0:T(8,128)(2,1)S(1)}, bf16[512,1536]{1,0:T(8,128)(2,1)}, u32[]{:S(2)}, u32[]{:S(2)}) collective-permute-start(bf16[512,1536]{1,0:T(8,128)(2,1)S(1)} %convolution_convert_fusion.2), channel_id=1, source_target_pairs={{0,16},{16,0},{1,17},{17,1},{2,18},{18,2},{3,19},{19,3},{4,20},{20... | collective-permute-start | bytes 4718600 | tf_op jit(solution)/shard_map/ppermute | solution.py:479
  255.4 39.0 %collective-permute-start.1 = (f32[512,1]{0,1:T(1,128)S(1)}, f32[512,1]{0,1:T(1,128)S(1)}, u32[]{:S(2)}, u32[]{:S(2)}) collective-permute-start(f32[512,1]{0,1:T(1,128)S(1)} %bitcast.294), channel_id=1, source_target_pairs={{0,16},{16,0},{1,17},{17,1},{2,18},{18,2},{3,19},{19,3},{4,20},{20... | collective-permute-start | bytes 6152 | tf_op jit(solution)/shard_map/ppermute | solution.py:479
  257.2 37.4 %collective-permute-start.4 = (f32[512,1]{0,1:T(1,128)S(1)}, f32[512,1]{0,1:T(1,128)S(1)}, u32[]{:S(2)}, u32[]{:S(2)}) collective-permute-start(f32[512,1]{0,1:T(1,128)S(1)} %bitcast.298), channel_id=1, source_target_pairs={{0,16},{16,0},{1,17},{17,1},{2,18},{18,2},{3,19},{19,3},{4,20},{20... | collective-permute-start | bytes 6152 | tf_op jit(solution)/shard_map/ppermute | solution.py:479
  338.4 85.2 %collective-permute-start.7 = (bf16[512,1536]{1,0:T(8,128)(2,1)}, bf16[512,1536]{1,0:T(8,128)(2,1)}, u32[]{:S(2)}, u32[]{:S(2)}) collective-permute-start(bf16[512,1536]{1,0:T(8,128)(2,1)} %convolution_convert_fusion.1), channel_id=1, source_target_pairs={{0,16},{16,0},{1,17},{17,1},{2,18},{18,2},{3,19},{19,3},{4,20},{20... | collective-permute-start | bytes 4718600 | tf_op jit(solution)/shard_map/ppermute | solution.py:479
  339.6 36.4 %collective-permute-start.6 = (f32[512,1]{0,1:T(1,128)S(1)}, f32[512,1]{0,1:T(1,128)S(1)}, u32[]{:S(2)}, u32[]{:S(2)}) collective-permute-start(f32[512,1]{0,1:T(1,128)S(1)} %bitcast.292), channel_id=1, source_target_pairs={{0,16},{16,0},{1,17},{17,1},{2,18},{18,2},{3,19},{19,3},{4,20},{20... | collective-permute-start | bytes 6152 | tf_op jit(solution)/shard_map/ppermute | solution.py:479
  365.9 57.8 %slice-start.2 = ((s8[6291456]{0:T(1024)(128)(4,1)}), s8[2097152]{0:T(1024)(128)(4,1)S(1)}, s32[]{:S(2)}) async-start(s8[6291456]{0:T(1024)(128)(4,1)} %bitcast.262), calls=%async_computation.17 | async-start | bytes 4194304
  369.6 54.0 %collective-permute-start.9 = (bf16[512,1536]{1,0:T(8,128)(2,1)}, bf16[512,1536]{1,0:T(8,128)(2,1)}, u32[]{:S(2)}, u32[]{:S(2)}) collective-permute-start(bf16[512,1536]{1,0:T(8,128)(2,1)} %convolution_convert_fusion), channel_id=1, source_target_pairs={{0,16},{16,0},{1,17},{17,1},{2,18},{18,2},{3,19},{19,3},{4,20},{20... | collective-permute-start | bytes 4718600 | tf_op jit(solution)/shard_map/ppermute | solution.py:479
  370.8 37.0 %collective-permute-start.8 = (f32[512,1]{0,1:T(1,128)S(1)}, f32[512,1]{0,1:T(1,128)S(1)}, u32[]{:S(2)}, u32[]{:S(2)}) collective-permute-start(f32[512,1]{0,1:T(1,128)S(1)} %bitcast.296), channel_id=1, source_target_pairs={{0,16},{16,0},{1,17},{17,1},{2,18},{18,2},{3,19},{19,3},{4,20},{20... | collective-permute-start | bytes 6152 | tf_op jit(solution)/shard_map/ppermute | solution.py:479
  517.2 282.6 %reduce-scatter.5.cloned.1.call-start = ((), (), s32[]{:S(2)}) async-start(), calls=%async_computation.8 | async-start | bytes 13762560 | tf_op jit(solution)/shard_map/reduce_scatter | solution.py:584
  517.3 81.3 %slice-start.4 = ((s8[6291456]{0:T(1024)(128)(4,1)}), s8[4194304]{0:T(1024)(128)(4,1)S(1)}, s32[]{:S(2)}) async-start(s8[6291456]{0:T(1024)(128)(4,1)} %bitcast.264), calls=%async_computation.19 | async-start | bytes 8388608
  527.4 71.1 %slice-start.5 = ((s8[6291456]{0:T(1024)(128)(4,1)}), s8[2097152]{0:T(1024)(128)(4,1)S(1)}, s32[]{:S(2)}) async-start(s8[6291456]{0:T(1024)(128)(4,1)} %bitcast.264), calls=%async_computation.20 | async-start | bytes 4194304
  527.5 37.3 %collective-permute-start.10 = (bf16[512,1536]{1,0:T(8,128)(2,1)S(1)}, bf16[512,1536]{1,0:T(8,128)(2,1)S(1)}, u32[]{:S(2)}, u32[]{:S(2)}) collective-permute-start(bf16[512,1536]{1,0:T(8,128)(2,1)S(1)} %fusion.46), channel_id=1, source_target_pairs={{0,16},{16,0},{1,17},{17,1},{2,18},{18,2},{3,19},{19,3},{4,20},{20... | collective-permute-start | bytes 4718600 | tf_op jit(solution)/shard_map/ppermute | solution.py:479
  539.7 58.9 %copy-start.32 = (bf16[512,1536]{1,0:T(8,128)(2,1)S(1)}, bf16[512,1536]{1,0:T(8,128)(2,1)}, u32[]{:S(2)}) copy-start(bf16[512,1536]{1,0:T(8,128)(2,1)} %copy-done.31) | copy-start | bytes 4718596
  539.7 56.4 %collective-permute-start.12 = (bf16[512,1536]{1,0:T(8,128)(2,1)S(1)}, bf16[512,1536]{1,0:T(8,128)(2,1)S(1)}, u32[]{:S(2)}, u32[]{:S(2)}) collective-permute-start(bf16[512,1536]{1,0:T(8,128)(2,1)S(1)} %fusion.52), channel_id=1, source_target_pairs={{0,16},{16,0},{1,17},{17,1},{2,18},{18,2},{3,19},{19,3},{4,20},{20... | collective-permute-start | bytes 4718600 | tf_op jit(solution)/shard_map/ppermute | solution.py:479
  615.7 30.0 %copy-start.39 = (bf16[512,1536]{1,0:T(8,128)(2,1)S(1)}, bf16[512,1536]{1,0:T(8,128)(2,1)}, u32[]{:S(2)}) copy-start(bf16[512,1536]{1,0:T(8,128)(2,1)} %get-tuple-element.153) | copy-start | bytes 4718596
  645.7 36.6 %slice-start = ((s8[6291456]{0:T(1024)(128)(4,1)}), s8[4194304]{0:T(1024)(128)(4,1)S(1)}, s32[]{:S(2)}) async-start(s8[6291456]{0:T(1024)(128)(4,1)} %bitcast.260), calls=%async_computation.15 | async-start | bytes 8388608
  709.8 140.8 %reduce-scatter.11.cloned.1.call-start = ((), (), s32[]{:S(2)}) async-start(), calls=%async_computation.11 | async-start | bytes 5898240 | tf_op jit(solution)/shard_map/reduce_scatter | solution.py:587
  722.8 178.7 %reduce-scatter.9.cloned.1.call-start = ((), (), s32[]{:S(2)}) async-start(), calls=%async_computation.10 | async-start | bytes 5898240 | tf_op jit(solution)/shard_map/reduce_scatter | solution.py:587
  734.0 265.1 %all-reduce.20.cloned.1.call-start = ((), (), s32[]{:S(2)}) async-start(), calls=%async_computation.13 | async-start | bytes 262144 | tf_op jit(solution)/shard_map/psum | solution.py:591
  753.3 152.1 %copy-start.33 = (bf16[512,1536]{1,0:T(8,128)(2,1)}, bf16[512,1536]{1,0:T(8,128)(2,1)S(1)}, u32[]{:S(2)}) copy-start(bf16[512,1536]{1,0:T(8,128)(2,1)S(1)} %fusion.49) | copy-start | bytes 4718596
  753.3 152.1 %collective-permute-start.11 = (bf16[512,1536]{1,0:T(8,128)(2,1)S(1)}, bf16[512,1536]{1,0:T(8,128)(2,1)S(1)}, u32[]{:S(2)}, u32[]{:S(2)}) collective-permute-start(bf16[512,1536]{1,0:T(8,128)(2,1)S(1)} %fusion.49), channel_id=1, source_target_pairs={{0,16},{16,0},{1,17},{17,1},{2,18},{18,2},{3,19},{19,3},{4,20},{20... | collective-permute-start | bytes 4718600 | tf_op jit(solution)/shard_map/ppermute | solution.py:479
  761.7 143.7 %collective-permute-start.13 = (bf16[512,1536]{1,0:T(8,128)(2,1)}, bf16[512,1536]{1,0:T(8,128)(2,1)}, u32[]{:S(2)}, u32[]{:S(2)}) collective-permute-start(bf16[512,1536]{1,0:T(8,128)(2,1)} %fusion.55), channel_id=1, source_target_pairs={{0,16},{16,0},{1,17},{17,1},{2,18},{18,2},{3,19},{19,3},{4,20},{20... | collective-permute-start | bytes 4718600 | tf_op jit(solution)/shard_map/ppermute | solution.py:479
  803.5 131.9 %collective-permute-start.14 = (bf16[384,3584]{1,0:T(8,128)(2,1)}, bf16[384,3584]{1,0:T(8,128)(2,1)}, u32[]{:S(2)}, u32[]{:S(2)}) collective-permute-start(bf16[384,3584]{1,0:T(8,128)(2,1)} %broadcast_select_fusion.2), channel_id=1, source_target_pairs={{0,16},{16,0},{1,17},{17,1},{2,18},{18,2},{3,19},{19,3},{4,20},{20... | collective-permute-start | bytes 8257544 | tf_op jit(solution)/shard_map/ppermute | solution.py:479
  903.9 27.8 %collective-permute-start.15 = (bf16[384,1536]{1,0:T(8,128)(2,1)}, bf16[384,1536]{1,0:T(8,128)(2,1)}, u32[]{:S(2)}, u32[]{:S(2)}) collective-permute-start(bf16[384,1536]{1,0:T(8,128)(2,1)} %broadcast_select_fusion.11), channel_id=1, source_target_pairs={{0,16},{16,0},{1,17},{17,1},{2,18},{18,2},{3,19},{19,3},{4,20},{20... | collective-permute-start | bytes 3538952 | tf_op jit(solution)/shard_map/ppermute | solution.py:479
  911.4 350.3 %all-reduce.22.cloned.1.call-start = ((), (), s32[]{:S(2)}) async-start(), calls=%async_computation.14 | async-start | bytes 14745600 | tf_op jit(solution)/shard_map/psum | solution.py:599
  1000.0 7.6 collective-permute-start.16
  (64 other events, 548.9 us)
Sparse Core Ops, SparseCore 0:
  41.7 51.7 all-reduce.17
  911.6 87.5 all-reduce.19
  1002.2 259.5 all-reduce.21
Sparse Core Ops, SparseCore 1:
  105.3 73.5 all-gather.5
  180.3 37.3 all-gather.7
  219.1 73.0 all-gather.9
  293.7 37.3 all-gather.11
  517.3 87.9 reduce-scatter.6
  709.9 89.9 reduce-scatter.4
  802.8 47.8 reduce-scatter.10
  853.6 47.8 reduce-scatter.8
